TPU v7x, 512 devices: a whole 4x8x8 slice. The times are simulated.
512 devices in a mesh: seq: 128 (over y, z, core), head: 4 (over x).
Axes of the slice: x: 4, y: 8, z: 8, core: 2. Of those that a mesh axis runs over, the one named last changes fastest.
Arguments:
- queries: bfloat16 [65536, 2048], P('seq', 'head'), may hold values from -4 to 4
- keys: bfloat16 [65536, 2048], P('seq', 'head'), may hold values from -4 to 4
- values: bfloat16 [65536, 2048], P('seq', 'head'), may hold values from -6 to 6
- rates: float32 [65536, 4], P('seq', 'head'), may hold values from 0.02 to 0.3
- fast: bfloat16 [4, 3, 512, 512], P('head'), may hold values from -0.25 to 0.25
- momentum: float32 [4, 3, 512, 512], P('head', None, 'seq'), may hold values from -0.24 to 0.24
- out_proj: bfloat16 [2048, 2048], P('seq', 'head'), may hold values from -0.125 to 0.125
Outputs:
- mixed: bfloat16 [65536, 2048], P('seq', 'head')
- new_momentum: float32 [4, 3, 512, 512], P('head', None, 'seq')
All inputs are finite; a program needn't handle non-finite values.
Results may differ from a plain program's by a relative error of at most 0.0094.
Values may be sent and summed in bfloat16 or wider, within the bound.
A program may use at most 64 MiB of HBM per device.

v0:
```python
import math

import jax
import jax.numpy as jnp
from jax import lax
from jax.sharding import PartitionSpec as P

HD = 512
WINDOW = 512


MOMENTUM_DECAY = 0.9
NORM_EPS = 1e-06
NEG_LARGE = -1e30


def from_behind(array, axis, by):
    devices = lax.axis_size(axis)
    pairs = [(i, i + by) for i in range(devices) if 0 <= i + by < devices]
    return lax.ppermute(array, axis, pairs)


def times_transposed(left, right):
    return lax.dot_general(
        left, right, (((1,), (1,)), ((), ())), preferred_element_type=jnp.float32
    )


def contract_rows(left, right):
    return lax.dot_general(
        left, right, (((0,), (0,)), ((), ())), preferred_element_type=jnp.float32
    )


def renormalize(base, moment):
    updated = base - moment
    base_rms = jnp.sqrt(jnp.mean(base * base, axis=-1, keepdims=True) + NORM_EPS)
    new_rms = jnp.sqrt(jnp.mean(updated * updated, axis=-1, keepdims=True) + NORM_EPS)
    return (updated * (base_rms / new_rms)).astype(jnp.bfloat16)


def shards(queries, keys, values, rates, fast, momentum, out_proj):
    tok_rows = queries.shape[0]
    ranks = lax.axis_size("seq")
    position = lax.axis_index("seq")
    own_rows = momentum.shape[2]
    grad_scale = 1.0 / math.sqrt(tok_rows * ranks)
    weights = fast[0]
    h_gate = times_transposed(keys, weights[0])
    h_up = times_transposed(keys, weights[1])
    sigma = jax.nn.sigmoid(h_gate)
    gated = (h_gate * sigma * h_up).astype(jnp.bfloat16)
    errors = (-grad_scale * rates * values.astype(jnp.float32)).astype(jnp.bfloat16)
    grad_down = contract_rows(errors, gated)
    back = jnp.dot(errors, weights[2], preferred_element_type=jnp.float32)
    d_gate = (back * h_up * sigma * (1.0 + h_gate * (1.0 - sigma))).astype(jnp.bfloat16)
    d_up = (back * h_gate * sigma).astype(jnp.bfloat16)
    grad_gate = contract_rows(d_gate, keys)
    grad_up = contract_rows(d_up, keys)
    grads = jnp.stack([grad_gate, grad_up, grad_down])
    row_start = position * own_rows
    placed = lax.dynamic_update_slice_in_dim(
        jnp.zeros(grads.shape, jnp.float32), MOMENTUM_DECAY * momentum[0], row_start, 1
    )
    moment_full = lax.psum(grads + placed, "seq")
    renewed = renormalize(weights.astype(jnp.float32), moment_full)
    moment_own = lax.dynamic_slice_in_dim(moment_full, row_start, own_rows, 1)
    q_gate = times_transposed(queries, renewed[0])
    q_up = times_transposed(queries, renewed[1])
    fast_in = (q_gate * jax.nn.sigmoid(q_gate) * q_up).astype(jnp.bfloat16)
    fast_out = times_transposed(fast_in, renewed[2])
    reach = (WINDOW + tok_rows - 2) // tok_rows
    stacked = jnp.stack([keys, values])
    earlier = [from_behind(stacked, "seq", 1)]
    extended = jnp.concatenate(earlier + [stacked], axis=1)
    key_count = extended.shape[1]
    key_pos = (position - reach) * tok_rows + jnp.arange(key_count)
    block = min(512, tok_rows)
    query_pos = position * tok_rows + 0 + jnp.arange(block)
    spacing = query_pos[:, None] - key_pos[None, :]
    allowed = (spacing >= 0) & (spacing < WINDOW) & (key_pos[None, :] >= 0)
    scores = times_transposed(queries, extended[0]) * (1.0 / math.sqrt(HD))
    scores = jnp.where(allowed, scores, NEG_LARGE)
    highest = jnp.max(scores, axis=1, keepdims=True)
    expo = jnp.exp(scores - highest)
    probs = (expo / jnp.sum(expo, axis=1, keepdims=True)).astype(jnp.bfloat16)
    attended_parts = jnp.dot(probs, extended[1], preferred_element_type=jnp.float32)
    combined = (attended_parts + fast_out).astype(jnp.bfloat16)
    all_heads = lax.all_gather(combined, "head", axis=1, tiled=True)
    projected = jnp.dot(
        all_heads,
        lax.all_gather(out_proj, "seq", axis=0, tiled=True),
        preferred_element_type=jnp.float32,
    )
    return (projected.astype(jnp.bfloat16), moment_own[None])


def solution(mesh):
    return jax.shard_map(
        shards,
        mesh=mesh,
        in_specs=(
            P("seq", "head"),
            P("seq", "head"),
            P("seq", "head"),
            P("seq", "head"),
            P("head", None, None, None),
            P("head", None, "seq", None),
            P("seq", "head"),
        ),
        out_specs=(P("seq", "head"), P("head", None, "seq", None)),
        check_vma=False,
    )
```

profile of v0, /device:TPU:1, one launch (start us, length us, event | category | flops | bytes accessed | tf_op | source)
XLA Modules:
  0.0 359.7 jit_solution(3982330911854318718)
XLA Ops:
  7.2 0.0 copy-start
  7.2 0.0 copy-start.1
  7.2 0.0 copy-start.3
  7.2 0.0 all-reduce.2.cloned.1.call-start
  7.2 0.0 copy-start.10
  7.3 0.0 copy-start.4
  7.3 1.8 fusion.14
  9.1 0.0 copy-done.1
  9.1 0.0 copy-done.3
  9.1 0.5 fusion.16
  9.6 0.0 copy-done.10
  9.6 0.0 copy-done.4
  9.6 0.5 fusion.18
  10.1 1.6 convolution_bitcast_fusion.2
  11.7 1.8 convolution_bitcast_fusion.4
  13.5 1.5 convolution_bitcast_fusion.3
  15.0 3.9 %pad_maximum_fusion = f32[3,512,512]{2,1,0:T(8,128)} fusion(f32[1,512,512]{2,1,0:T(8,128)} %convolution_bitcast_fusion.2, f32[1,512,512]{2,1,0:T(8,128)} %convolution_bitcast_fusion.3, f32[1,512,512]{2,1,0:T(8,128)} %convolution_bitcast_fusion.4), kind=kLoop, calls=%fused_computation.3 | loop fusion | flops 1572864 | bytes 6291456 | tf_op jit(solution)/shard_map/stack | solution.py:60
  18.9 0.0 copy-done.9
  18.9 1.4 fusion.26
  20.3 0.0 all-reduce.2.cloned.1.call-update
  20.3 0.0 all-gather.5.cloned.1.call-start
  20.4 0.7 all-gather.5.cloned.1.call-update
  21.1 0.0 all-gather.3.cloned.1.call-start
  21.1 1.2 pad_maximum_fusion.1
  22.3 5.4 %collective-permute-start = (bf16[2,512,512]{2,1,0:T(8,128)(2,1)}, bf16[2,512,512]{2,1,0:T(8,128)(2,1)}, u32[]{:S(2)}, u32[]{:S(2)}) collective-permute-start(bf16[2,512,512]{2,1,0:T(8,128)(2,1)} %pad_maximum_fusion.1), channel_id=1, source_target_pairs={{0,4},{4,8},{8,12},{12,16},{16,20},{20,24},{24,28},{28,32},{32,36}... | collective-permute-start | bytes 3145736 | tf_op jit(solution)/shard_map/ppermute | solution.py:20
  27.7 12.2 %collective-permute-done = bf16[2,512,512]{2,1,0:T(8,128)(2,1)} collective-permute-done((bf16[2,512,512]{2,1,0:T(8,128)(2,1)}, bf16[2,512,512]{2,1,0:T(8,128)(2,1)}, u32[]{:S(2)}, u32[]{:S(2)}) %collective-permute-start) | collective-permute-done | bytes 1048608 | tf_op jit(solution)/shard_map/ppermute | solution.py:20
  39.9 1.4 maximum_maximum_fusion
  41.3 0.0 copy-done
  41.3 0.0 copy-start.6
  41.3 1.1 fusion.31
  42.5 0.2 copy-done.6
  42.7 1.3 copy-done.8
  44.0 0.4 fusion.3
  44.4 185.0 %all-reduce.2.cloned.1.call-done = f32[3,512,512]{2,1,0:T(8,128)} async-done(((f32[3,512,512]{2,1,0:T(8,128)}), f32[3,512,512]{2,1,0:T(8,128)}) %all-reduce.2.cloned.1.call-update) | async-done | bytes 3145744 | tf_op jit(solution)/shard_map/psum | solution.py:65
  229.4 2.7 fusion
  232.2 0.1 copy-done.2
  232.3 0.4 multiply_convert_fusion
  232.7 0.0 copy-start.5
  232.7 1.2 copy-done.5
  233.8 1.5 convolution_bitcast_fusion.1
  235.3 3.5 fusion.7
  238.8 0.0 copy-done.7
  238.8 3.4 fusion.5
  242.2 0.0 all-gather.3.cloned.1.call-update
  242.2 1.4 dynamic-slice_bitcast_fusion
  243.7 70.2 %all-gather.5.cloned.1.call-done = bf16[2048,512]{1,0:T(8,128)(2,1)} async-done(((bf16[16,512]{1,0:T(8,128)(2,1)}), bf16[2048,512]{1,0:T(8,128)(2,1)}) %all-gather.5.cloned.1.call-update) | async-done | bytes 2097168 | tf_op jit(solution)/shard_map/all_gather | solution.py:92
  313.8 35.1 %all-gather.3.cloned.1.call-done = bf16[512,2048]{1,0:T(8,128)(2,1)} async-done(((bf16[512,512]{1,0:T(8,128)(2,1)}), bf16[512,2048]{1,0:T(8,128)(2,1)}) %all-gather.3.cloned.1.call-update) | async-done | bytes 2097168 | tf_op jit(solution)/shard_map/all_gather | solution.py:89
  348.9 4.3 %convolution_convert_fusion = bf16[512,512]{1,0:T(8,128)(2,1)} fusion(bf16[512,2048]{1,0:T(8,128)(2,1)} %all-gather.3.cloned.1.call-done, bf16[2048,512]{1,0:T(8,128)(2,1)} %all-gather.5.cloned.1.call-done), kind=kOutput, calls=%fused_computation.23 | convolution fusion | flops 1074003968 | bytes 4718592 | tf_op jit(solution)/shard_map/dot_general | solution.py:90
  (9 shorter events, 0.0 us)
Async XLA Ops:
  7.2 34.1 %copy-start = (bf16[512,512]{1,0:T(8,128)(2,1)S(1)}, bf16[512,512]{1,0:T(8,128)(2,1)}, u32[]{:S(2)}) copy-start(bf16[512,512]{1,0:T(8,128)(2,1)} %param.7) | copy-start | bytes 1572868
  7.2 1.9 copy-start.1
  7.2 1.9 copy-start.3
  7.2 222.2 %all-reduce.2.cloned.1.call-start = ((), (), s32[]{:S(2)}) async-start(), calls=%async_computation | async-start | bytes 6291456 | tf_op jit(solution)/shard_map/psum | solution.py:65
  7.2 2.3 copy-start.10
  7.3 2.3 copy-start.4
  15.0 3.9 %copy-start.9 = (f32[1,3,4,512]{3,2,1,0:T(4,128)S(1)}, f32[1,3,4,512]{3,2,1,0:T(4,128)}, u32[]{:S(2)}) copy-start(f32[1,3,4,512]{3,2,1,0:T(4,128)} %param.12) | copy-start | bytes 73732
  20.3 293.5 %all-gather.5.cloned.1.call-start = ((), (), s32[]{:S(2)}) async-start(), calls=%async_computation.2 | async-start | bytes 2113536 | tf_op jit(solution)/shard_map/all_gather | solution.py:92
  21.1 327.8 %all-gather.3.cloned.1.call-start = ((), (), s32[]{:S(2)}) async-start(), calls=%async_computation.1 | async-start | bytes 2621440 | tf_op jit(solution)/shard_map/all_gather | solution.py:89
  22.3 17.6 %collective-permute-start = (bf16[2,512,512]{2,1,0:T(8,128)(2,1)}, bf16[2,512,512]{2,1,0:T(8,128)(2,1)}, u32[]{:S(2)}, u32[]{:S(2)}) collective-permute-start(bf16[2,512,512]{2,1,0:T(8,128)(2,1)} %pad_maximum_fusion.1), channel_id=1, source_target_pairs={{0,4},{4,8},{8,12},{12,16},{16,20},{20,24},{24,28},{28,32},{32,36}... | collective-permute-start | bytes 3145736 | tf_op jit(solution)/shard_map/ppermute | solution.py:20
  41.3 1.4 copy-start.6
  42.7 1.3 copy-start.8
  229.4 2.8 copy-start.2
  232.7 1.2 copy-start.5
  235.3 3.5 copy-start.7
Sparse Core Ops, SparseCore 0:
  20.5 208.9 all-reduce.1
  232.5 81.2 all-gather.4
  316.5 32.3 all-gather.2
where the time goes:
time: 360 us
  waiting for transfers between devices  303 us (84%)
  matrix products  21.5 us (6%)
  between operations  13.9 us (4%)
  other arithmetic  11.3 us (3%)
  starting transfers between devices  5.49 us (2%)
  local copies, waits for them, and re-layouts  4.24 us (1%)
    psum x1, waiting for transfers between devices, shards(): moment_full = lax.psum(grads + placed, 'seq')  185 us
    all_gather x1, waiting for transfers between devices, shards(): lax.all_gather(out_proj, 'seq', axis=0, tiled=True)  70.2 us
    all_gather x1, waiting for transfers between devices, shards(): all_heads = lax.all_gather(combined, 'head', axis=1, tiled=True)  35.1 us
    ppermute x1, waiting for transfers between devices, from_behind(): return lax.ppermute(array, axis, pairs)  12.2 us
    dot_general x5, matrix products, times_transposed(): lax.dot_general(left, right, (((1,), (1,)), ((), ())), preferred_element_...  8.38 us
  transfers between devices with their start and end apart: 4, of which 4 were waited for; matrix products, arithmetic and copies ran while one was open for 5% of the time, Pallas kernels for 0%

commit v1 on v0

v1 whole, which is shorter than its diff:
```python
import functools
import math

import jax
import jax.numpy as jnp
from jax import lax
from jax.experimental import pallas as pl
from jax.experimental.pallas import tpu as pltpu
from jax.sharding import PartitionSpec as P

MOMENTUM_DECAY = 0.9
NORM_EPS = 1e-06
NEG_LARGE = -1e30
LANES = 128
MESH = pl.DeviceIdType.MESH
F32 = jnp.float32
BF16 = jnp.bfloat16


def nt(left, right):
    return lax.dot_general(left, right, (((1,), (1,)), ((), ())), preferred_element_type=F32)


def nn(left, right):
    return lax.dot_general(left, right, (((1,), (0,)), ((), ())), preferred_element_type=F32)


def tn(left, right):
    return lax.dot_general(left, right, (((0,), (0,)), ((), ())), preferred_element_type=F32)


def layer_kernel(
    side, heads, grad_scale,
    q_hbm, k_hbm, v_hbm, rates_ref, fast_hbm, mom_ref, proj_hbm,
    out_ref, newmom_ref,
    q_ref, fast_ref, ext_k, ext_v, err_t, grads, gbuf, exbuf, s1buf, r1buf, s2buf, r2buf,
    fin, sibfin, mompad, sibmom, rbuf, renewed, wbuf, wnat, att, comb, acc,
    load_sem, ex_send, ex_recv, kv_send, kv_recv, mom_send, mom_recv,
    a_send, a_recv, b_send, b_recv, fin_send, fin_recv,
    g1_send, g1_recv, g2_send, g2_recv, gs_send, gs_recv,
    w1_send, w1_recv, w2_send, w2_recv, ws_send, ws_recv,
    x_send, x_recv, f_send, f_recv,
):
    tok = q_ref.shape[0]
    hd = q_ref.shape[1]
    half = hd // 2
    blocks = half // LANES
    chips = side * side
    rows = hd // chips
    own_rows = rows // 2
    tall = rows * blocks

    seq = lax.axis_index("seq")
    head = lax.axis_index("head")
    core = lax.rem(seq, 2)
    chip = lax.div(seq, 2)
    y = lax.div(chip, side)
    z = lax.rem(chip, side)
    a1 = y + core * (z - y)
    a2 = z + core * (y - z)
    ranks = 2 * chips

    def along(d, first):
        use_y = (1 - core) if first else core
        py = lax.rem(y + d * use_y, side)
        pz = lax.rem(z + d * (1 - use_y), side)
        return ((py * side + pz) * 2 + core, head)

    def coord(d, first):
        return lax.rem((a1 if first else a2) + d, side)

    sibling = (chip * 2 + 1 - core, head)
    after = (lax.rem(seq + 1, ranks), head)
    right = (seq, lax.rem(head + 1, heads))
    left = (seq, lax.rem(head + heads - 1, heads))
    far = (lax.rem(seq + 2 * core - 1 + ranks, ranks), head)

    def remote(src, dst, send, recv, device):
        return pltpu.make_async_remote_copy(
            src_ref=src, dst_ref=dst, send_sem=send, recv_sem=recv,
            device_id=device, device_id_type=MESH,
        )

    barrier = pltpu.get_barrier_semaphore()

    def greet(d, _):
        pl.semaphore_signal(barrier, inc=1, device_id=along(d, True), device_id_type=MESH)
        pl.semaphore_signal(barrier, inc=1, device_id=along(d, False), device_id_type=MESH)
        return 0

    lax.fori_loop(1, side, greet, 0)
    for device in (sibling, right, left, far):
        pl.semaphore_signal(barrier, inc=1, device_id=device, device_id_type=MESH)

    loads = [
        pltpu.make_async_copy(k_hbm, ext_k.at[pl.ds(tok, tok)], load_sem.at[0]),
        pltpu.make_async_copy(fast_hbm, fast_ref, load_sem.at[1]),
        pltpu.make_async_copy(v_hbm, ext_v.at[pl.ds(tok, tok)], load_sem.at[2]),
        pltpu.make_async_copy(q_hbm, q_ref, load_sem.at[3]),
        pltpu.make_async_copy(proj_hbm, wbuf.at[core, a1, a2], load_sem.at[4]),
    ]
    for load in loads:
        load.start()

    row_of = lax.broadcasted_iota(jnp.int32, (rows, hd), 0)
    for m in range(3):
        padded = jnp.zeros((rows, hd), F32)
        for r in range(own_rows):
            value = MOMENTUM_DECAY * mom_ref[0, m, r:r + 1, :]
            padded = jnp.where(row_of == r + own_rows * core, jnp.broadcast_to(value, (rows, hd)), padded)
        mompad[m] = padded

    loads[2].wait()
    rate_row = -grad_scale * rates_ref[...]
    err_t[...] = (rate_row * ext_v[tok:, :].astype(F32).T).astype(BF16)
    loads[0].wait()
    loads[1].wait()
    hid = min(256, hd)

    def gradient(i, _):
        part = pl.ds(pl.multiple_of(i * hid, hid), hid)
        keys = ext_k[tok:, :]
        gate = nt(fast_ref[0, 0, part, :], keys)
        up = nt(fast_ref[0, 1, part, :], keys)
        sigma = jax.nn.sigmoid(gate)
        gated = (gate * sigma * up).astype(BF16)
        back = tn(fast_ref[0, 2, :, part], err_t[...])
        d_gate = (back * up * sigma * (1.0 + gate * (1.0 - sigma))).astype(BF16)
        d_up = (back * gate * sigma).astype(BF16)
        grads[0, part, :] = nn(d_gate, keys)
        grads[1, part, :] = nn(d_up, keys)
        grads[2, :, part] = nt(err_t[...], gated)
        return 0

    lax.fori_loop(0, hd // hid, gradient, 0)

    def pack(i, _):
        m = lax.div(i, side)
        py = lax.rem(i, side)
        line = grads[m, pl.ds(pl.multiple_of(py * side * rows, side * rows), side * rows), :]
        line = line.reshape(side, rows, hd)
        for h in range(2):
            pieces = [
                line[:, :, h * half + b * LANES:h * half + (b + 1) * LANES] for b in range(blocks)
            ]
            tile = (jnp.concatenate(pieces, axis=1) if blocks > 1 else pieces[0]).astype(BF16)
            if h == 0:
                gbuf[0, m, py] = tile
            else:
                gbuf[1, m, :, py] = tile
        return 0

    lax.fori_loop(0, 3 * side, pack, 0)

    pl.semaphore_wait(barrier, 2 * (side - 1) + 4)

    exchange = [
        remote(gbuf.at[1 - core, m], exbuf.at[m], ex_send.at[m], ex_recv.at[m], sibling)
        for m in range(3)
    ]
    for copy in exchange:
        copy.start()
    mom_copy = remote(mompad, sibmom, mom_send, mom_recv, sibling)
    mom_copy.start()

    def stage_a(m, d):
        return remote(
            s1buf.at[m, coord(d, True)], r1buf.at[m, d - 1],
            a_send.at[m, d - 1], a_recv.at[m, d - 1], along(d, True),
        )

    def stage_b(d):
        return remote(
            s2buf.at[coord(d, False)], r2buf.at[d - 1],
            b_send.at[d - 1], b_recv.at[d - 1], along(d, False),
        )

    def each(fn):
        lax.fori_loop(1, side, lambda d, _: (fn(d), 0)[1], 0)

    for m in range(3):
        exchange[m].wait_recv()
        s1buf[m] = (gbuf[core, m].astype(F32) + exbuf[m].astype(F32)).astype(BF16)
        each(lambda d, m=m: stage_a(m, d).start())

    loads[4].wait()

    def w_first(d):
        spot = wbuf.at[core, a1, a2]
        return remote(spot, spot, w1_send.at[d - 1], w1_recv.at[d - 1], along(d, False))

    def w_second(d):
        slab = wbuf.at[core, a1]
        return remote(slab, slab, w2_send.at[d - 1], w2_recv.at[d - 1], along(d, True))

    each(lambda d: w_first(d).start())
    kv = [
        remote(ext.at[pl.ds(tok, tok)], ext.at[pl.ds(0, tok)], kv_send.at[i], kv_recv.at[i], after)
        for i, ext in enumerate((ext_k, ext_v))
    ]
    for copy in kv:
        copy.start()

    for m in range(3):
        each(lambda d, m=m: stage_a(m, d).wait_recv())
        total = s1buf[m, a1].astype(F32)
        for d in range(side - 1):
            total = total + r1buf[m, d].astype(F32)
        s2buf[:, m] = total.astype(BF16)
    each(lambda d: stage_b(d).start())
    each(lambda d: stage_b(d).wait_recv())
    total = s2buf[a2].astype(F32)
    for d in range(side - 1):
        total = total + r2buf[d].astype(F32)
    fin[...] = total
    fin_copy = remote(fin, sibfin, fin_send, fin_recv, sibling)
    fin_copy.start()
    mom_copy.wait_recv()
    fin_copy.wait_recv()

    pair = max(1, 16 // rows)
    base_row = pl.multiple_of(lax.div(chip, pair) * (pair * rows), pair * rows)
    for m in range(3):
        mine, other = fin[m], sibfin[m]
        lanes = []
        for h in range(2):
            use = jnp.where(core == h, mine, other)
            lanes += [use[b * rows:(b + 1) * rows] for b in range(blocks)]
        moment = jnp.concatenate(lanes, axis=1) + (mompad[m] + sibmom[m])
        for r in range(own_rows):
            newmom_ref[0, m, r:r + 1, :] = jnp.where(
                core == 0, moment[r:r + 1], moment[own_rows + r:own_rows + r + 1]
            )
        wide = fast_ref[0, m, pl.ds(base_row, pair * rows), :].astype(F32)
        base = wide[:rows]
        for p in range(1, pair):
            base = jnp.where(lax.rem(chip, pair) == p, wide[p * rows:(p + 1) * rows], base)
        updated = base - moment
        base_rms = jnp.sqrt(jnp.mean(base * base, axis=-1, keepdims=True) + NORM_EPS)
        new_rms = jnp.sqrt(jnp.mean(updated * updated, axis=-1, keepdims=True) + NORM_EPS)
        fresh = updated * (base_rms / new_rms)
        fresh = jnp.where(core == 0, fresh[:, :half], fresh[:, half:])
        parts = [fresh[:, b * LANES:(b + 1) * LANES] for b in range(blocks)]
        packed = jnp.concatenate(parts, axis=0) if blocks > 1 else parts[0]
        rbuf[core, a1, a2, m] = packed.astype(BF16)

    def g_first(d):
        spot = rbuf.at[core, a1, a2]
        return remote(spot, spot, g1_send.at[d - 1], g1_recv.at[d - 1], along(d, False))

    def g_second(d):
        slab = rbuf.at[core, a1]
        return remote(slab, slab, g2_send.at[d - 1], g2_recv.at[d - 1], along(d, True))

    def g_sib(d):
        slab = rbuf.at[core, coord(side - d, True)]
        return remote(slab, slab, gs_send.at[d], gs_recv.at[d], sibling)

    each(lambda d: g_first(d).start())
    each(lambda d: g_first(d).wait_recv())
    each(lambda d: g_second(d).start())
    g_sib(0).start()

    each(lambda d: w_first(d).wait_recv())
    each(lambda d: w_second(d).start())

    loads[3].wait()
    for copy in kv:
        copy.wait_recv()
    chunk = tok // 4
    span = tok + chunk
    scale = 1.0 / math.sqrt(hd)
    q_local = lax.broadcasted_iota(jnp.int32, (chunk, span), 0)
    k_local = lax.broadcasted_iota(jnp.int32, (chunk, span), 1)
    window = (k_local > q_local) & (k_local <= q_local + tok)

    def attend(i, _):
        part = pl.ds(pl.multiple_of(i * chunk, chunk), chunk)
        reach = pl.ds(pl.multiple_of(i * chunk, chunk), span)
        first_key = jnp.where(seq == 0, tok, 0) - i * chunk
        scores = nt(q_ref[part, :], ext_k[reach, :]) * scale
        scores = jnp.where(window & (k_local >= first_key), scores, NEG_LARGE)
        highest = jnp.max(scores, axis=1, keepdims=True)
        expo = jnp.exp(scores - highest)
        total = jnp.sum(expo, axis=1, keepdims=True)
        att[part, :] = nn(expo.astype(BF16), ext_v[reach, :]) / total
        return 0

    lax.fori_loop(0, 4, attend, 0)

    def relay(d):
        g_second(d).wait_recv()
        g_sib(d).start()

    each(relay)
    lax.fori_loop(0, side, lambda d, _: (g_sib(d).wait_recv(), 0)[1], 0)

    def unpack(py, _):
        for m in range(3):
            lanes = []
            for h in range(2):
                tile = (rbuf[0, py, :, m] if h == 0 else rbuf[1, :, py, m]).astype(F32)
                lanes += [
                    tile[:, b * rows:(b + 1) * rows].reshape(side * rows, LANES) for b in range(blocks)
                ]
            place = pl.ds(pl.multiple_of(py * side * rows, side * rows), side * rows)
            renewed[m, place, :] = jnp.concatenate(lanes, axis=1).astype(BF16)
        return 0

    lax.fori_loop(0, side, unpack, 0)

    def to_right(i):
        piece = comb.at[head, pl.ds(pl.multiple_of(i * chunk, chunk), chunk)]
        return remote(piece, piece, x_send.at[0, i], x_recv.at[0, i], right)

    def to_left(i):
        piece = comb.at[head, pl.ds(pl.multiple_of(i * chunk, chunk), chunk)]
        return remote(piece, piece, x_send.at[1, i], x_recv.at[1, i], left)

    def forward(i, way):
        source = lax.rem(head + (heads - 1 if way == 0 else 1), heads)
        piece = comb.at[source, pl.ds(pl.multiple_of(i * chunk, chunk), chunk)]
        return remote(piece, piece, f_send.at[i], f_recv.at[i], right if way == 0 else left)

    def produce(n, _):
        i = 2 * lax.rem(n, 2) + lax.div(n, 2)
        part = pl.ds(pl.multiple_of(i * chunk, chunk), chunk)
        gate = nt(q_ref[part, :], renewed[0])
        up = nt(q_ref[part, :], renewed[1])
        fast_in = (gate * jax.nn.sigmoid(gate) * up).astype(BF16)
        fast_out = nt(fast_in, renewed[2])
        comb[head, part, :] = (att[part, :] + fast_out).astype(BF16)
        to_right(i).start()
        to_left(i).start()
        return 0

    lax.fori_loop(0, 4, produce, 0)

    each(lambda d: w_second(d).wait_recv())
    w_sib = remote(wbuf.at[core], wbuf.at[core], ws_send, ws_recv, sibling)
    w_sib.start()
    w_sib.wait_recv()
    w_rows = wbuf.shape[3]

    def natural(py, _):
        for pz in range(side):
            start = pl.multiple_of((py * side + pz) * 2 * w_rows, 2 * w_rows)
            wnat[pl.ds(start, w_rows), :] = wbuf[0, py, pz]
            wnat[pl.ds(start + w_rows, w_rows), :] = wbuf[1, pz, py]
        return 0

    lax.fori_loop(0, side, natural, 0)

    def project(source, i, first=False, last=False):
        part = pl.ds(pl.multiple_of(i * chunk, chunk), chunk)
        slab = wnat[pl.ds(pl.multiple_of(source * hd, hd), hd), :]
        value = nn(comb[source, part, :], slab)
        if not first:
            value = acc[part, :] + value
        if last:
            out_ref[part, :] = value.astype(BF16)
        else:
            acc[part, :] = value

    lax.fori_loop(0, 4, lambda i, _: (project(head, i, first=True), 0)[1], 0)

    from_left = lax.rem(head + heads - 1, heads)
    from_right = lax.rem(head + 1, heads)
    opposite = lax.rem(head + 2, heads)

    def neighbours(n, _):
        low = n
        high = n + 2
        to_right(low).wait_recv()
        forward(low, 0).start()
        to_left(low).wait_recv()
        project(from_left, low)
        project(from_right, low)
        to_left(high).wait_recv()
        forward(high, 1).start()
        to_right(high).wait_recv()
        project(from_left, high)
        project(from_right, high)
        return 0

    lax.fori_loop(0, 2, neighbours, 0)

    def finish(n, _):
        forward(n, 0).wait_recv()
        project(opposite, n, last=True)
        forward(n + 2, 1).wait_recv()
        project(opposite, n + 2, last=True)
        return 0

    lax.fori_loop(0, 2, finish, 0)

    for copy in exchange + kv + [mom_copy, fin_copy, w_sib]:
        copy.wait_send()

    def drain(d):
        for m in range(3):
            stage_a(m, d).wait_send()
        stage_b(d).wait_send()
        g_first(d).wait_send()
        g_second(d).wait_send()
        w_first(d).wait_send()
        w_second(d).wait_send()

    each(drain)
    lax.fori_loop(0, side, lambda d, _: (g_sib(d).wait_send(), 0)[1], 0)

    def drain_x(n, _):
        for i in (n, n + 2):
            to_right(i).wait_send()
            to_left(i).wait_send()
        forward(n, 0).wait_send()
        forward(n + 2, 1).wait_send()
        return 0

    lax.fori_loop(0, 2, drain_x, 0)


def shards(side, queries, keys, values, rates, fast, momentum, out_proj):
    tok, hd = queries.shape
    heads = lax.axis_size("head")
    ranks = lax.axis_size("seq")
    half = hd // 2
    blocks = half // LANES
    rows = hd // (side * side)
    tall = rows * blocks
    w_rows = out_proj.shape[0]
    grad_scale = 1.0 / math.sqrt(tok * ranks)
    dma = pltpu.SemaphoreType.DMA
    peers = side - 1
    anywhere = pl.BlockSpec(memory_space=pl.ANY)
    vmem = pl.BlockSpec(memory_space=pltpu.VMEM)
    return tuple(pl.pallas_call(
        functools.partial(layer_kernel, side, heads, grad_scale),
        out_shape=(
            jax.ShapeDtypeStruct((tok, hd), BF16),
            jax.ShapeDtypeStruct(momentum.shape, F32),
        ),
        in_specs=[anywhere, anywhere, anywhere, vmem, anywhere, vmem, anywhere],
        out_specs=(vmem, vmem),
        scratch_shapes=[
            pltpu.VMEM((tok, hd), BF16),
            pltpu.VMEM((1, 3, hd, hd), BF16),
            pltpu.VMEM((2 * tok, hd), BF16),
            pltpu.VMEM((2 * tok, hd), BF16),
            pltpu.VMEM((hd, tok), BF16),
            pltpu.VMEM((3, hd, hd), F32),
            pltpu.VMEM((2, 3, side, side, tall, LANES), BF16),
            pltpu.VMEM((3, side, side, tall, LANES), BF16),
            pltpu.VMEM((3, side, side, tall, LANES), BF16),
            pltpu.VMEM((3, peers, side, tall, LANES), BF16),
            pltpu.VMEM((side, 3, tall, LANES), BF16),
            pltpu.VMEM((peers, 3, tall, LANES), BF16),
            pltpu.VMEM((3, tall, LANES), F32),
            pltpu.VMEM((3, tall, LANES), F32),
            pltpu.VMEM((3, rows, hd), F32),
            pltpu.VMEM((3, rows, hd), F32),
            pltpu.VMEM((2, side, side, 3, tall, LANES), BF16),
            pltpu.VMEM((3, hd, hd), BF16),
            pltpu.VMEM((2, side, side, w_rows, hd), BF16),
            pltpu.VMEM((heads * hd, hd), BF16),
            pltpu.VMEM((tok, hd), F32),
            pltpu.VMEM((heads, tok, hd), BF16),
            pltpu.VMEM((tok, hd), F32),
            dma((5,)), dma((3,)), dma((3,)), dma((2,)), dma((2,)), dma(()), dma(()),
            dma((3, peers)), dma((3, peers)), dma((peers,)), dma((peers,)), dma(()), dma(()),
            dma((peers,)), dma((peers,)), dma((peers,)), dma((peers,)), dma((side,)), dma((side,)),
            dma((peers,)), dma((peers,)), dma((peers,)), dma((peers,)), dma(()), dma(()),
            dma((2, 4)), dma((2, 4)), dma((4,)), dma((4,)),
        ],
        compiler_params=pltpu.CompilerParams(
            collective_id=0, has_side_effects=True, vmem_limit_bytes=56 * 1024 * 1024,
        ),
    )(queries, keys, values, rates.reshape(1, tok), fast, momentum, out_proj))


def solution(mesh):
    side = math.isqrt(mesh.shape["seq"] // 2)
    return jax.shard_map(
        functools.partial(shards, side),
        mesh=mesh,
        in_specs=(
            P("seq", "head"),
            P("seq", "head"),
            P("seq", "head"),
            P("seq", "head"),
            P("head", None, None, None),
            P("head", None, "seq", None),
            P("seq", "head"),
        ),
        out_specs=(P("seq", "head"), P("head", None, "seq", None)),
        check_vma=False,
    )
```

time: 360 us -> 93.2 us (0.26)
  waiting for transfers between devices: 303 us -> 0 us
  Pallas kernels: 0 us -> 88.9 us
  matrix products: 21.5 us -> 0 us
  between operations: 13.9 us -> 0.64 us
  other arithmetic: 11.3 us -> 0 us
  starting transfers between devices: 5.49 us -> 0 us
    psum x1 -> x0, waiting for transfers between devices: 185 us -> none  [shards(): moment_full = lax.psum(grads + placed, 'seq')]
    all_gather x2 -> x0, waiting for transfers between devices: 105 us -> none  [the longest x1 70.2 us: shards(): lax.all_gather(out_proj, 'seq', axis=0, tiled=True)]
    pallas_call x0 -> x1, Pallas kernels: none -> 88.9 us  [shards(): pl.pallas_call(functools.partial(layer_kernel, side, heads, grad_scale),...]
    dot_general x11 -> x0, matrix products: 21.5 us -> none  [the longest x5 8.38 us: times_transposed(): lax.dot_general(left, right, (((1,), (1,)), ((), ())), preferred_element_...]
    ppermute x1 -> x0, waiting for transfers between devices: 12.2 us -> none  [from_behind(): return lax.ppermute(array, axis, pairs)]
    ppermute x1 -> x0, starting transfers between devices: 5.38 us -> none  [from_behind(): return lax.ppermute(array, axis, pairs)]
    another operation x2 -> x0, other arithmetic: 5.02 us -> none  [the longest x1 3.86 us: shards(): grads = jnp.stack([grad_gate, grad_up, grad_down])]
  transfers between devices with their start and end apart: 4 -> 0, of which waited for: 4 -> 0; matrix products, arithmetic and copies ran while one was open for 5% -> 0% of each run, Pallas kernels for 0% -> 0%
where the time goes in v1:
time: 93.2 us; the launch traced here: 92.8 us
  Pallas kernels  88.9 us (95%)
  local copies, waits for them, and re-layouts  3.21 us (3%)
    pallas_call x1, Pallas kernels, shards(): pl.pallas_call(functools.partial(layer_kernel, side, heads, grad_scale),...  88.9 us
    unnamed x2, local copies, waits for them, and re-layouts  3.21 us

profile of v1, /device:TPU:1, one launch (start us, length us, event | category | flops | bytes accessed | tf_op | source)
XLA Modules:
  0.0 92.8 jit_solution(17103726111616963589)
XLA Ops:
  0.6 88.9 %shard_map.86 = (bf16[512,512]{1,0:T(8,128)(2,1)}, f32[1,3,4,512]{3,2,1,0:T(4,128)}) custom-call(bf16[512,512]{1,0:T(8,128)(2,1)} %q_hbm.1, bf16[512,512]{1,0:T(8,128)(2,1)} %k_hbm.1, bf16[512,512]{1,0:T(8,128)(2,1)} %v_hbm.1, f32[1,512]{1,0:T(1,128)} %bitcast.1, bf16[1,3,512,512]{3,2,1,0:T(8,128)(2,1)} %fast_hbm.1, f32[1,3,4,512]{3,2,1,0:T(4,128)} %mom_ref.1, ...), custom_call_target="tpu_custom_call" | custom-call | tf_op jit(solution)/shard_map/pallas_call | solution.py:437
  89.6 1.9 %copy.11 = bf16[512,512]{1,0:T(8,128)(2,1)} copy(bf16[512,512]{1,0:T(8,128)(2,1)} %get-tuple-element.4) | data formatting | bytes 1048576
  91.4 1.3 %copy.12 = f32[1,3,4,512]{3,2,1,0:T(4,128)} copy(f32[1,3,4,512]{3,2,1,0:T(4,128)} %get-tuple-element.5) | data formatting | bytes 49152

commit v2 on v1

--- a/solution.py
+++ b/solution.py
@@ -31,12 +31,12 @@
 
 def layer_kernel(
     side, heads, grad_scale,
-    q_hbm, k_hbm, v_hbm, rates_ref, fast_hbm, mom_ref, proj_hbm,
+    q_hbm, k_hbm, v_hbm, rates_hbm, fast_hbm, mom_hbm, proj_hbm,
     out_ref, newmom_ref,
-    q_ref, fast_ref, ext_k, ext_v, err_t, grads, gbuf, exbuf, s1buf, r1buf, s2buf, r2buf,
-    fin, sibfin, mompad, sibmom, rbuf, renewed, wbuf, wnat, att, comb, acc,
+    rates_ref, mom_ref, q_ref, fast_ref, ext_k, ext_v, err_t, grads, gbuf, exbuf, s1buf, r1buf, rhalf, aggbuf, s2buf, r2buf,
+    r2sib, mompad, sibmom, rbuf, renewed, wbuf, wnat, att, comb, acc,
     load_sem, ex_send, ex_recv, kv_send, kv_recv, mom_send, mom_recv,
-    a_send, a_recv, b_send, b_recv, fin_send, fin_recv,
+    a_send, a_recv, b_send, b_recv, c_send, c_recv,
     g1_send, g1_recv, g2_send, g2_recv, gs_send, gs_recv,
     w1_send, w1_recv, w2_send, w2_recv, ws_send, ws_recv,
     x_send, x_recv, f_send, f_recv,
@@ -60,14 +60,11 @@
     a2 = z + core * (y - z)
     ranks = 2 * chips
 
-    def along(d, first):
+    def along(d, first, swap=False):
         use_y = (1 - core) if first else core
         py = lax.rem(y + d * use_y, side)
         pz = lax.rem(z + d * (1 - use_y), side)
-        return ((py * side + pz) * 2 + core, head)
-
-    def coord(d, first):
-        return lax.rem((a1 if first else a2) + d, side)
+        return ((py * side + pz) * 2 + (1 - core if swap else core), head)
 
     sibling = (chip * 2 + 1 - core, head)
     after = (lax.rem(seq + 1, ranks), head)
@@ -80,17 +77,6 @@
             src_ref=src, dst_ref=dst, send_sem=send, recv_sem=recv,
             device_id=device, device_id_type=MESH,
         )
-
-    barrier = pltpu.get_barrier_semaphore()
-
-    def greet(d, _):
-        pl.semaphore_signal(barrier, inc=1, device_id=along(d, True), device_id_type=MESH)
-        pl.semaphore_signal(barrier, inc=1, device_id=along(d, False), device_id_type=MESH)
-        return 0
-
-    lax.fori_loop(1, side, greet, 0)
-    for device in (sibling, right, left, far):
-        pl.semaphore_signal(barrier, inc=1, device_id=device, device_id_type=MESH)
 
     loads = [
         pltpu.make_async_copy(k_hbm, ext_k.at[pl.ds(tok, tok)], load_sem.at[0]),
@@ -98,10 +84,148 @@
         pltpu.make_async_copy(v_hbm, ext_v.at[pl.ds(tok, tok)], load_sem.at[2]),
         pltpu.make_async_copy(q_hbm, q_ref, load_sem.at[3]),
         pltpu.make_async_copy(proj_hbm, wbuf.at[core, a1, a2], load_sem.at[4]),
+        pltpu.make_async_copy(mom_hbm, mom_ref, load_sem.at[5]),
+        pltpu.make_async_copy(rates_hbm, rates_ref, load_sem.at[6]),
     ]
-    for load in loads:
+    for load in (loads[0], loads[1], loads[2], loads[6], loads[5], loads[4], loads[3]):
         load.start()
 
+    barrier = pltpu.get_barrier_semaphore()
+
+    def greet(d, _):
+        for first in (True, False):
+            for swap in (True, False):
+                device = along(d, first, swap)
+                pl.semaphore_signal(barrier, inc=1, device_id=device, device_id_type=MESH)
+        return 0
+
+    lax.fori_loop(1, side, greet, 0)
+    for device in (sibling, right, left, far):
+        pl.semaphore_signal(barrier, inc=1, device_id=device, device_id_type=MESH)
+
+    for load in (loads[0], loads[1], loads[2], loads[6]):
+        load.wait()
+
+    def gradient(i, first):
+        part = pl.ds(pl.multiple_of(i * half, half), half)
+        keys = ext_k[tok:, :]
+        gate = nt(fast_ref[0, 0, part, :], keys)
+        up = nt(fast_ref[0, 1, part, :], keys)
+        if first:
+            rate_row = -grad_scale * rates_ref[...]
+            err_t[...] = (rate_row * ext_v[tok:, :].astype(F32).T).astype(BF16)
+        sigma = jax.nn.sigmoid(gate)
+        gated = (gate * sigma * up).astype(BF16)
+        back = tn(fast_ref[0, 2, :, part], err_t[...])
+        grads[2, :, part] = nt(err_t[...], gated)
+        d_gate = (back * up * sigma * (1.0 + gate * (1.0 - sigma))).astype(BF16)
+        d_up = (back * gate * sigma).astype(BF16)
+        grads[0, part, :] = nn(d_gate, keys)
+        grads[1, part, :] = nn(d_up, keys)
+
+    def pieces_of(m, py, h):
+        line = grads[m, pl.ds(pl.multiple_of(py * side * rows, side * rows), side * rows), h * half:(h + 1) * half]
+        line = line.reshape(side, rows, half)
+        parts = [line[:, :, b * LANES:(b + 1) * LANES] for b in range(blocks)]
+        tile = (jnp.concatenate(parts, axis=1) if blocks > 1 else parts[0]).astype(BF16)
+        if h == 0:
+            gbuf[0, m, py] = tile
+        else:
+            gbuf[1, m, :, py] = tile
+
+    def pack_rows(i):
+        def body(n, _):
+            for m in range(2):
+                for h in range(2):
+                    pieces_of(m, i * (side // 2) + n, h)
+            return 0
+
+        lax.fori_loop(0, side // 2, body, 0)
+
+    def pack_down(i):
+        for h in range(2):
+            @pl.when(i == h)
+            def _():
+                lax.fori_loop(0, side, lambda n, _: (pieces_of(2, n, h), 0)[1], 0)
+
+    def ex_down():
+        return remote(gbuf.at[1 - core, 2], exbuf.at[2], ex_send.at[4], ex_recv.at[4], sibling)
+
+    def ex_part(m, p, c):
+        where = (1 - c, m, pl.ds(p * (side // 2), side // 2))
+        if c == 0:
+            where = (1 - c, m, slice(None), pl.ds(p * (side // 2), side // 2))
+        return remote(
+            gbuf.at[where], exbuf.at[where[1:]], ex_send.at[2 * m + p], ex_recv.at[2 * m + p], sibling
+        )
+
+    def ex_parts(mine):
+        for c in range(2):
+            p = c if mine else 1 - c
+
+            @pl.when(core == c)
+            def _():
+                for m in range(2):
+                    ex_part(m, p, c).start()
+
+    def each(fn):
+        lax.fori_loop(1, side, lambda d, _: (fn(d), 0)[1], 0)
+
+    def w_first(d):
+        spot = wbuf.at[core, a1, a2]
+        return remote(spot, spot, w1_send.at[d - 1], w1_recv.at[d - 1], along(d, False))
+
+    ways = ((side - 1, 0), (1, 1))
+
+    def half_of(w):
+        return pl.ds(w * (side // 2), side // 2)
+
+    def coord(d, first):
+        return lax.rem((a1 if first else a2) + d, side)
+
+    def second(buf, send, recv, kind, d, w):
+        back = side - d
+        if kind == 0:
+            slab, reach = buf.at[core, a1], 2 * d
+        elif kind == 1:
+            slab, reach = buf.at[core, a1], d
+        elif kind == 2:
+            slab, reach = buf.at[core, coord(2 * back, True)], d
+        else:
+            slab, reach = buf.at[core, coord(2 * back, True), half_of(w)], 2 * d
+        return remote(slab, slab, send.at[kind, w], recv.at[kind, w], along(reach, True))
+
+    def w_second(kind, d, w):
+        return second(wbuf, w2_send, w2_recv, kind, d, w)
+
+    def w_sib(n):
+        slab = wbuf.at[core, coord(n, True)]
+        return remote(slab, slab, ws_send.at[n], ws_recv.at[n], sibling)
+
+    gradient(1 - core, True)
+    pl.semaphore_wait(barrier, 4 * (side - 1) + 4)
+    kv_rows = tok // 4
+    kv = [
+        remote(
+            ext.at[pl.ds(tok + n * kv_rows, kv_rows)], ext.at[pl.ds(n * kv_rows, kv_rows)],
+            kv_send.at[i, n], kv_recv.at[i, n], after,
+        )
+        for i, ext in enumerate((ext_k, ext_v)) for n in range(4)
+    ]
+    for copy in kv[:2]:
+        copy.start()
+    loads[4].wait()
+    each(lambda d: w_first(d).start())
+    pack_down(1 - core)
+    pack_rows(1 - core)
+    ex_down().start()
+    ex_parts(False)
+    gradient(core, False)
+
+    pack_rows(core)
+    ex_parts(True)
+    pack_down(core)
+    loads[5].wait()
     row_of = lax.broadcasted_iota(jnp.int32, (rows, hd), 0)
     for m in range(3):
         padded = jnp.zeros((rows, hd), F32)
@@ -110,121 +234,94 @@
             padded = jnp.where(row_of == r + own_rows * core, jnp.broadcast_to(value, (rows, hd)), padded)
         mompad[m] = padded
 
-    loads[2].wait()
-    rate_row = -grad_scale * rates_ref[...]
-    err_t[...] = (rate_row * ext_v[tok:, :].astype(F32).T).astype(BF16)
-    loads[0].wait()
-    loads[1].wait()
-    hid = min(256, hd)
-
-    def gradient(i, _):
-        part = pl.ds(pl.multiple_of(i * hid, hid), hid)
-        keys = ext_k[tok:, :]
-        gate = nt(fast_ref[0, 0, part, :], keys)
-        up = nt(fast_ref[0, 1, part, :], keys)
-        sigma = jax.nn.sigmoid(gate)
-        gated = (gate * sigma * up).astype(BF16)
-        back = tn(fast_ref[0, 2, :, part], err_t[...])
-        d_gate = (back * up * sigma * (1.0 + gate * (1.0 - sigma))).astype(BF16)
-        d_up = (back * gate * sigma).astype(BF16)
-        grads[0, part, :] = nn(d_gate, keys)
-        grads[1, part, :] = nn(d_up, keys)
-        grads[2, :, part] = nt(err_t[...], gated)
-        return 0
-
-    lax.fori_loop(0, hd // hid, gradient, 0)
-
-    def pack(i, _):
-        m = lax.div(i, side)
-        py = lax.rem(i, side)
-        line = grads[m, pl.ds(pl.multiple_of(py * side * rows, side * rows), side * rows), :]
-        line = line.reshape(side, rows, hd)
-        for h in range(2):
-            pieces = [
-                line[:, :, h * half + b * LANES:h * half + (b + 1) * LANES] for b in range(blocks)
-            ]
-            tile = (jnp.concatenate(pieces, axis=1) if blocks > 1 else pieces[0]).astype(BF16)
-            if h == 0:
-                gbuf[0, m, py] = tile
-            else:
-                gbuf[1, m, :, py] = tile
-        return 0
-
-    lax.fori_loop(0, 3 * side, pack, 0)
-
-    pl.semaphore_wait(barrier, 2 * (side - 1) + 4)
-
-    exchange = [
-        remote(gbuf.at[1 - core, m], exbuf.at[m], ex_send.at[m], ex_recv.at[m], sibling)
-        for m in range(3)
-    ]
-    for copy in exchange:
-        copy.start()
     mom_copy = remote(mompad, sibmom, mom_send, mom_recv, sibling)
     mom_copy.start()
 
-    def stage_a(m, d):
+    def a_relay(m, d, w):
         return remote(
-            s1buf.at[m, coord(d, True)], r1buf.at[m, d - 1],
-            a_send.at[m, d - 1], a_recv.at[m, d - 1], along(d, True),
-        )
-
-    def stage_b(d):
+            s1buf.at[m, coord(3 * d, True)], r1buf.at[m, w, 0],
+            a_send.at[m, w, 0], a_recv.at[m, w, 0], along(d, True),
+        )
+
+    def a_half(m, d, w):
         return remote(
-            s2buf.at[coord(d, False)], r2buf.at[d - 1],
-            b_send.at[d - 1], b_recv.at[d - 1], along(d, False),
-        )
-
-    def each(fn):
-        lax.fori_loop(1, side, lambda d, _: (fn(d), 0)[1], 0)
-
-    for m in range(3):
-        exchange[m].wait_recv()
+            s1buf.at[m, coord(side // 2, True), half_of(w)], rhalf.at[m, w],
+            a_send.at[m, w, 1], a_recv.at[m, w, 1], along(2 * d, True),
+        )
+
+    def a_direct(m, d, w):
+        return remote(
+            s1buf.at[m, coord(d, True)], r1buf.at[m, w, 1],
+            a_send.at[m, w, 2], a_recv.at[m, w, 2], along(d, True),
+        )
+
+    def a_agg(m, d, w):
+        return remote(
+            aggbuf.at[m, w], r1buf.at[m, w, 2],
+            a_send.at[m, w, 3], a_recv.at[m, w, 3], along(2 * d, True),
+        )
+
+    def stage_b(d, swap):
+        send, recv = (c_send, c_recv) if swap else (b_send, b_recv)
+        return remote(
+            s2buf.at[coord(d, False)], (r2sib if swap else r2buf).at[d],
+            send.at[d], recv.at[d], along(d, False, swap),
+        )
+
+    order = (2, 0, 1)
+    for m in order:
+        if m == 2:
+            ex_down().wait_recv()
+        else:
+            for p in range(2):
+                ex_part(m, p, 1).wait_recv()
         s1buf[m] = (gbuf[core, m].astype(F32) + exbuf[m].astype(F32)).astype(BF16)
-        each(lambda d, m=m: stage_a(m, d).start())
-
-    loads[4].wait()
-
-    def w_first(d):
-        spot = wbuf.at[core, a1, a2]
-        return remote(spot, spot, w1_send.at[d - 1], w1_recv.at[d - 1], along(d, False))
-
-    def w_second(d):
-        slab = wbuf.at[core, a1]
-        return remote(slab, slab, w2_send.at[d - 1], w2_recv.at[d - 1], along(d, True))
-
-    each(lambda d: w_first(d).start())
-    kv = [
-        remote(ext.at[pl.ds(tok, tok)], ext.at[pl.ds(0, tok)], kv_send.at[i], kv_recv.at[i], after)
-        for i, ext in enumerate((ext_k, ext_v))
-    ]
-    for copy in kv:
+        for stage in (a_half, a_relay, a_direct):
+            for d, w in ways:
+                stage(m, d, w).start()
+
+    for copy in kv[2:4]:
         copy.start()
-
-    for m in range(3):
-        each(lambda d, m=m: stage_a(m, d).wait_recv())
+    for m in order:
+        for d, w in ways:
+            a_half(m, d, w).wait_recv()
+            a_relay(m, d, w).wait_recv()
+            total = s1buf[m, coord(2 * d, True)].astype(F32) + r1buf[m, w, 0].astype(F32)
+            aggbuf[m, w] = total.astype(BF16)
+            part = half_of(w)
+            total = s1buf[m, coord(2 * d, True), part].astype(F32)
+            total = total + r1buf[m, w, 0, part].astype(F32) + rhalf[m, w].astype(F32)
+            aggbuf[m, w, part] = total.astype(BF16)
+            a_agg(m, d, w).start()
+    for m in order:
         total = s1buf[m, a1].astype(F32)
-        for d in range(side - 1):
-            total = total + r1buf[m, d].astype(F32)
+        for stage, kind in ((a_direct, 1), (a_agg, 2)):
+            for d, w in ways:
+                stage(m, d, w).wait_recv()
+                total = total + r1buf[m, w, kind].astype(F32)
         s2buf[:, m] = total.astype(BF16)
-    each(lambda d: stage_b(d).start())
-    each(lambda d: stage_b(d).wait_recv())
-    total = s2buf[a2].astype(F32)
-    for d in range(side - 1):
-        total = total + r2buf[d].astype(F32)
-    fin[...] = total
-    fin_copy = remote(fin, sibfin, fin_send, fin_recv, sibling)
-    fin_copy.start()
+    def b_start(d):
+        stage_b(d, False).start()
+        stage_b(d, True).start()
+
+    each(b_start)
+    kv[4].start()
+    stage_b(0, True).start()
+    stage_b(0, True).wait_recv()
+    each(lambda d: stage_b(d, False).wait_recv())
+    each(lambda d: stage_b(d, True).wait_recv())
+    mine = s2buf[a2].astype(F32)
+    other = r2sib[0].astype(F32)
+    for d in range(1, side):
+        mine = mine + r2buf[d].astype(F32)
+        other = other + r2sib[d].astype(F32)
     mom_copy.wait_recv()
-    fin_copy.wait_recv()
-
     pair = max(1, 16 // rows)
     base_row = pl.multiple_of(lax.div(chip, pair) * (pair * rows), pair * rows)
     for m in range(3):
-        mine, other = fin[m], sibfin[m]
         lanes = []
         for h in range(2):
-            use = jnp.where(core == h, mine, other)
+            use = jnp.where(core == h, mine[m], other[m])
             lanes += [use[b * rows:(b + 1) * rows] for b in range(blocks)]
         moment = jnp.concatenate(lanes, axis=1) + (mompad[m] + sibmom[m])
         for r in range(own_rows):
@@ -248,22 +345,51 @@
         spot = rbuf.at[core, a1, a2]
         return remote(spot, spot, g1_send.at[d - 1], g1_recv.at[d - 1], along(d, False))
 
-    def g_second(d):
-        slab = rbuf.at[core, a1]
-        return remote(slab, slab, g2_send.at[d - 1], g2_recv.at[d - 1], along(d, True))
-
-    def g_sib(d):
-        slab = rbuf.at[core, coord(side - d, True)]
-        return remote(slab, slab, gs_send.at[d], gs_recv.at[d], sibling)
+    def g_second(kind, d, w):
+        return second(rbuf, g2_send, g2_recv, kind, d, w)
+
+    def g_sib(n):
+        slab = rbuf.at[core, coord(n, True)]
+        return remote(slab, slab, gs_send.at[n], gs_recv.at[n], sibling)
+
+    def spread(fn):
+        for kind in (0, 1):
+            for d, w in ways:
+                fn(kind, d, w).start()
+
+    def relay_far(fn):
+        for d, w in ways:
+            fn(0, d, w).wait_recv()
+            fn(3, d, w).start()
+            fn(2, d, w).start()
+
+    def hand_near(fn, sib):
+        sib(0).start()
+        for d, w in ways:
+            sib((side - 2 * d) % side).start()
+            fn(1, d, w).wait_recv()
+            sib(side - d).start()
+
+    def hand_far(fn, sib):
+        for d, w in ways:
+            fn(2, d, w).wait_recv()
+            sib((side - 3 * d) % side).start()
+        for d, w in ways:
+            fn(3, d, w).wait_recv()
+        sib(side // 2).start()
+
+    def await_sib(sib):
+        lax.fori_loop(0, side, lambda n, _: (sib(n).wait_recv(), 0)[1], 0)
 
     each(lambda d: g_first(d).start())
+    kv[5].start()
     each(lambda d: g_first(d).wait_recv())
-    each(lambda d: g_second(d).start())
-    g_sib(0).start()
-
-    each(lambda d: w_first(d).wait_recv())
-    each(lambda d: w_second(d).start())
-
+    spread(g_second)
+    for copy in kv[6:]:
+        copy.start()
+
+    relay_far(g_second)
+    hand_near(g_second, g_sib)
     loads[3].wait()
     for copy in kv:
         copy.wait_recv()
@@ -288,12 +414,10 @@
 
     lax.fori_loop(0, 4, attend, 0)
 
-    def relay(d):
-        g_second(d).wait_recv()
-        g_sib(d).start()
-
-    each(relay)
-    lax.fori_loop(0, side, lambda d, _: (g_sib(d).wait_recv(), 0)[1], 0)
+    hand_far(g_second, g_sib)
+    each(lambda d: w_first(d).wait_recv())
+    spread(w_second)
+    await_sib(g_sib)
 
     def unpack(py, _):
         for m in range(3):
@@ -336,10 +460,18 @@
 
     lax.fori_loop(0, 4, produce, 0)
 
-    each(lambda d: w_second(d).wait_recv())
-    w_sib = remote(wbuf.at[core], wbuf.at[core], ws_send, ws_recv, sibling)
-    w_sib.start()
-    w_sib.wait_recv()
+    def pass_on(n):
+        to_right(n).wait_recv()
+        forward(n, 0).start()
+        to_left(n + 2).wait_recv()
+        forward(n + 2, 1).start()
+
+    relay_far(w_second)
+    hand_near(w_second, w_sib)
+    pass_on(0)
+    hand_far(w_second, w_sib)
+    await_sib(w_sib)
+    pass_on(1)
     w_rows = wbuf.shape[3]
 
     def natural(py, _):
@@ -371,13 +503,9 @@
     def neighbours(n, _):
         low = n
         high = n + 2
-        to_right(low).wait_recv()
-        forward(low, 0).start()
         to_left(low).wait_recv()
         project(from_left, low)
         project(from_right, low)
-        to_left(high).wait_recv()
-        forward(high, 1).start()
         to_right(high).wait_recv()
         project(from_left, high)
         project(from_right, high)
@@ -394,20 +522,34 @@
 
     lax.fori_loop(0, 2, finish, 0)
 
-    for copy in exchange + kv + [mom_copy, fin_copy, w_sib]:
+    for copy in kv + [mom_copy, ex_down()]:
         copy.wait_send()
+    for m in range(2):
+        for p in range(2):
+            ex_part(m, p, 1).wait_send()
 
     def drain(d):
+        stage_b(d, False).wait_send()
+        stage_b(d, True).wait_send()
+        g_first(d).wait_send()
+        w_first(d).wait_send()
+
+    each(drain)
+    stage_b(0, True).wait_send()
+    for d, w in ways:
         for m in range(3):
-            stage_a(m, d).wait_send()
-        stage_b(d).wait_send()
-        g_first(d).wait_send()
-        g_second(d).wait_send()
-        w_first(d).wait_send()
-        w_second(d).wait_send()
-
-    each(drain)
-    lax.fori_loop(0, side, lambda d, _: (g_sib(d).wait_send(), 0)[1], 0)
+            for stage in (a_half, a_relay, a_direct, a_agg):
+                stage(m, d, w).wait_send()
+        for kind in range(4):
+            g_second(kind, d, w).wait_send()
+            w_second(kind, d, w).wait_send()
+
+    def drain_sib(d, _):
+        g_sib(d).wait_send()
+        w_sib(d).wait_send()
+        return 0
+
+    lax.fori_loop(0, side, drain_sib, 0)
 
     def drain_x(n, _):
         for i in (n, n + 2):
@@ -437,12 +579,14 @@
     return tuple(pl.pallas_call(
         functools.partial(layer_kernel, side, heads, grad_scale),
         out_shape=(
-            jax.ShapeDtypeStruct((tok, hd), BF16),
-            jax.ShapeDtypeStruct(momentum.shape, F32),
+            pltpu.VMEM((tok, hd), BF16),
+            pltpu.VMEM(momentum.shape, F32),
         ),
-        in_specs=[anywhere, anywhere, anywhere, vmem, anywhere, vmem, anywhere],
+        in_specs=[anywhere] * 7,
         out_specs=(vmem, vmem),
         scratch_shapes=[
+            pltpu.VMEM((1, tok), F32),
+            pltpu.VMEM(momentum.shape, F32),
             pltpu.VMEM((tok, hd), BF16),
             pltpu.VMEM((1, 3, hd, hd), BF16),
             pltpu.VMEM((2 * tok, hd), BF16),
@@ -452,11 +596,12 @@
             pltpu.VMEM((2, 3, side, side, tall, LANES), BF16),
             pltpu.VMEM((3, side, side, tall, LANES), BF16),
             pltpu.VMEM((3, side, side, tall, LANES), BF16),
-            pltpu.VMEM((3, peers, side, tall, LANES), BF16),
+            pltpu.VMEM((3, 2, 3, side, tall, LANES), BF16),
+            pltpu.VMEM((3, 2, side // 2, tall, LANES), BF16),
+            pltpu.VMEM((3, 2, side, tall, LANES), BF16),
             pltpu.VMEM((side, 3, tall, LANES), BF16),
-            pltpu.VMEM((peers, 3, tall, LANES), BF16),
-            pltpu.VMEM((3, tall, LANES), F32),
-            pltpu.VMEM((3, tall, LANES), F32),
+            pltpu.VMEM((side, 3, tall, LANES), BF16),
+            pltpu.VMEM((side, 3, tall, LANES), BF16),
             pltpu.VMEM((3, rows, hd), F32),
             pltpu.VMEM((3, rows, hd), F32),
             pltpu.VMEM((2, side, side, 3, tall, LANES), BF16),
@@ -466,10 +611,10 @@
             pltpu.VMEM((tok, hd), F32),
             pltpu.VMEM((heads, tok, hd), BF16),
             pltpu.VMEM((tok, hd), F32),
-            dma((5,)), dma((3,)), dma((3,)), dma((2,)), dma((2,)), dma(()), dma(()),
-            dma((3, peers)), dma((3, peers)), dma((peers,)), dma((peers,)), dma(()), dma(()),
-            dma((peers,)), dma((peers,)), dma((peers,)), dma((peers,)), dma((side,)), dma((side,)),
-            dma((peers,)), dma((peers,)), dma((peers,)), dma((peers,)), dma(()), dma(()),
+            dma((7,)), dma((5,)), dma((5,)), dma((2, 4)), dma((2, 4)), dma(()), dma(()),
+            dma((3, 2, 4)), dma((3, 2, 4)), dma((side,)), dma((side,)), dma((side,)), dma((side,)),
+            dma((peers,)), dma((peers,)), dma((4, 2)), dma((4, 2)), dma((side,)), dma((side,)),
+            dma((peers,)), dma((peers,)), dma((4, 2)), dma((4, 2)), dma((side,)), dma((side,)),
             dma((2, 4)), dma((2, 4)), dma((4,)), dma((4,)),
         ],
         compiler_params=pltpu.CompilerParams(

time: 93.2 us -> 78.2 us (0.84)
  Pallas kernels: 88.9 us -> 76.1 us
  local copies, waits for them, and re-layouts: 3.21 us -> 1.4 us
    pallas_call x1, Pallas kernels: 88.9 us -> 76.1 us  [shards(): pl.pallas_call(functools.partial(layer_kernel, side, heads, grad_scale),...]
    unnamed x2, local copies, waits for them, and re-layouts: 3.21 us -> 1.4 us
where the time goes in v2:
time: 78.2 us; the launch traced here: 78.1 us
  Pallas kernels  76.1 us (97%)
  local copies, waits for them, and re-layouts  1.4 us (2%)
    pallas_call x1, Pallas kernels, shards(): pl.pallas_call(functools.partial(layer_kernel, side, heads, grad_scale),...  76.1 us

profile of v2, /device:TPU:1, one launch (start us, length us, event | category | flops | bytes accessed | tf_op | source)
XLA Modules:
  0.0 78.1 jit_solution(11127755649924721624)
XLA Ops:
  0.6 76.1 %shard_map.86 = (bf16[512,512]{1,0:T(8,128)(2,1)S(1)}, f32[1,3,4,512]{3,2,1,0:T(4,128)S(1)}) custom-call(bf16[512,512]{1,0:T(8,128)(2,1)} %q_hbm.1, bf16[512,512]{1,0:T(8,128)(2,1)} %k_hbm.1, bf16[512,512]{1,0:T(8,128)(2,1)} %v_hbm.1, f32[1,512]{1,0:T(1,128)} %bitcast.1, bf16[1,3,512,512]{3,2,1,0:T(8,128)(2,1)} %fast_hbm.1, f32[1,3,4,512]{3,2,1,0:T(4,128)} %mom_hbm.1, ...), custom_call_target="tpu_custom_call" | custom-call | tf_op jit(solution)/shard_map/pallas_call | solution.py:579
  76.7 0.8 %copy.11 = bf16[512,512]{1,0:T(8,128)(2,1)} copy(bf16[512,512]{1,0:T(8,128)(2,1)S(1)} %get-tuple-element.2) | data formatting | bytes 1048576
  77.5 0.6 copy.12

commit v3 on v2

--- a/solution.py
+++ b/solution.py
@@ -13,6 +13,10 @@
 NEG_LARGE = -1e30
 LANES = 128
 MESH = pl.DeviceIdType.MESH
+PLACE = {7: 0, 0: 1, 1: 2, 2: 3, 6: 4, 3: 5, 4: 6, 5: 7}
+GROUPS = ((0, 3), (3, 2), (5, 3))
+GROUP_STEPS = (2, 2, 3)
+ACROSS = (((0, 3), None), ((3, 1), (4, 1)), (None, (5, 3)))
 F32 = jnp.float32
 BF16 = jnp.bfloat16
 
@@ -34,12 +38,9 @@
     q_hbm, k_hbm, v_hbm, rates_hbm, fast_hbm, mom_hbm, proj_hbm,
     out_ref, newmom_ref,
     rates_ref, mom_ref, q_ref, fast_ref, ext_k, ext_v, err_t, grads, gbuf, exbuf, s1buf, r1buf, rhalf, aggbuf, s2buf, r2buf,
-    r2sib, mompad, sibmom, rbuf, renewed, wbuf, wnat, att, comb, acc,
-    load_sem, ex_send, ex_recv, kv_send, kv_recv, mom_send, mom_recv,
-    a_send, a_recv, b_send, b_recv, c_send, c_recv,
-    g1_send, g1_recv, g2_send, g2_recv, gs_send, gs_recv,
-    w1_send, w1_recv, w2_send, w2_recv, ws_send, ws_recv,
-    x_send, x_recv, f_send, f_recv,
+    r2sib, mompad, sibmom, rbuf, renewed, wbuf, wnat, att, comb, acc, ebuf, sums, outbuf, mombuf,
+    load_sem, send_sem, ex_recv, kv_recv, mom_recv, ar_recv, ad_recv, b_recv, c_recv,
+    g1_recv, gr_recv, gs_recv, w1_recv, w2_recv, ws_recv, x_recv, f_recv, out_sem,
 ):
     tok = q_ref.shape[0]
     hd = q_ref.shape[1]
@@ -89,6 +90,9 @@
     ]
     for load in (loads[0], loads[1], loads[2], loads[6], loads[5], loads[4], loads[3]):
         load.start()
+
+    def await_bytes(ref, sem):
+        remote(ref, ref, send_sem.at[0], sem, sibling).wait_recv()
 
     barrier = pltpu.get_barrier_semaphore()
 
@@ -149,14 +153,14 @@
                 lax.fori_loop(0, side, lambda n, _: (pieces_of(2, n, h), 0)[1], 0)
 
     def ex_down():
-        return remote(gbuf.at[1 - core, 2], exbuf.at[2], ex_send.at[4], ex_recv.at[4], sibling)
+        return remote(gbuf.at[1 - core, 2], exbuf.at[2], send_sem.at[0], ex_recv.at[2], sibling)
 
     def ex_part(m, p, c):
         where = (1 - c, m, pl.ds(p * (side // 2), side // 2))
         if c == 0:
             where = (1 - c, m, slice(None), pl.ds(p * (side // 2), side // 2))
         return remote(
-            gbuf.at[where], exbuf.at[where[1:]], ex_send.at[2 * m + p], ex_recv.at[2 * m + p], sibling
+            gbuf.at[where], exbuf.at[where[1:]], send_sem.at[0], ex_recv.at[m], sibling
         )
 
     def ex_parts(mine):
@@ -173,7 +177,7 @@
 
     def w_first(d):
         spot = wbuf.at[core, a1, a2]
-        return remote(spot, spot, w1_send.at[d - 1], w1_recv.at[d - 1], along(d, False))
+        return remote(spot, spot, send_sem.at[3], w1_recv, along(d, False))
 
     ways = ((side - 1, 0), (1, 1))
 
@@ -183,7 +187,8 @@
     def coord(d, first):
         return lax.rem((a1 if first else a2) + d, side)
 
-    def second(buf, send, recv, kind, d, w):
+    def w_second(kind, d, w):
+        buf = wbuf
         back = side - d
         if kind == 0:
             slab, reach = buf.at[core, a1], 2 * d
@@ -193,14 +198,12 @@
             slab, reach = buf.at[core, coord(2 * back, True)], d
         else:
             slab, reach = buf.at[core, coord(2 * back, True), half_of(w)], 2 * d
-        return remote(slab, slab, send.at[kind, w], recv.at[kind, w], along(reach, True))
-
-    def w_second(kind, d, w):
-        return second(wbuf, w2_send, w2_recv, kind, d, w)
+        spot = (w, 2 + w, 4 + w, 6)[kind]
+        return remote(slab, slab, send_sem.at[3], w2_recv.at[spot], along(reach, True))
 
     def w_sib(n):
         slab = wbuf.at[core, coord(n, True)]
-        return remote(slab, slab, ws_send.at[n], ws_recv.at[n], sibling)
+        return remote(slab, slab, send_sem.at[4], ws_recv, sibling)
 
     gradient(1 - core, True)
     pl.semaphore_wait(barrier, 4 * (side - 1) + 4)
@@ -208,7 +211,7 @@
     kv = [
         remote(
             ext.at[pl.ds(tok + n * kv_rows, kv_rows)], ext.at[pl.ds(n * kv_rows, kv_rows)],
-            kv_send.at[i, n], kv_recv.at[i, n], after,
+            send_sem.at[1], kv_recv.at[i], after,
         )
         for i, ext in enumerate((ext_k, ext_v)) for n in range(4)
     ]
@@ -234,58 +237,54 @@
             padded = jnp.where(row_of == r + own_rows * core, jnp.broadcast_to(value, (rows, hd)), padded)
         mompad[m] = padded
 
-    mom_copy = remote(mompad, sibmom, mom_send, mom_recv, sibling)
+    mom_copy = remote(mompad, sibmom, send_sem.at[0], mom_recv, sibling)
     mom_copy.start()
 
     def a_relay(m, d, w):
         return remote(
             s1buf.at[m, coord(3 * d, True)], r1buf.at[m, w, 0],
-            a_send.at[m, w, 0], a_recv.at[m, w, 0], along(d, True),
+            send_sem.at[0], ar_recv.at[m, w], along(d, True),
         )
 
     def a_half(m, d, w):
         return remote(
             s1buf.at[m, coord(side // 2, True), half_of(w)], rhalf.at[m, w],
-            a_send.at[m, w, 1], a_recv.at[m, w, 1], along(2 * d, True),
+            send_sem.at[0], ar_recv.at[m, w], along(2 * d, True),
         )
 
     def a_direct(m, d, w):
         return remote(
             s1buf.at[m, coord(d, True)], r1buf.at[m, w, 1],
-            a_send.at[m, w, 2], a_recv.at[m, w, 2], along(d, True),
+            send_sem.at[0], ad_recv.at[m], along(d, True),
         )
 
     def a_agg(m, d, w):
         return remote(
             aggbuf.at[m, w], r1buf.at[m, w, 2],
-            a_send.at[m, w, 3], a_recv.at[m, w, 3], along(2 * d, True),
+            send_sem.at[0], ad_recv.at[m], along(2 * d, True),
         )
 
     def stage_b(d, swap):
-        send, recv = (c_send, c_recv) if swap else (b_send, b_recv)
+        send, recv = (send_sem.at[0], c_recv) if swap else (send_sem.at[2], b_recv)
         return remote(
             s2buf.at[coord(d, False)], (r2sib if swap else r2buf).at[d],
-            send.at[d], recv.at[d], along(d, False, swap),
+            send, recv, along(d, False, swap),
         )
 
     order = (2, 0, 1)
     for m in order:
-        if m == 2:
-            ex_down().wait_recv()
-        else:
-            for p in range(2):
-                ex_part(m, p, 1).wait_recv()
+        await_bytes(exbuf.at[m], ex_recv.at[m])
         s1buf[m] = (gbuf[core, m].astype(F32) + exbuf[m].astype(F32)).astype(BF16)
-        for stage in (a_half, a_relay, a_direct):
+        for stage in (a_half, a_relay):
             for d, w in ways:
                 stage(m, d, w).start()
-
-    for copy in kv[2:4]:
-        copy.start()
     for m in order:
         for d, w in ways:
-            a_half(m, d, w).wait_recv()
-            a_relay(m, d, w).wait_recv()
+            a_direct(m, d, w).start()
+
+    for m in order:
+        for d, w in ways:
+            await_bytes(rhalf.at[:, 0], ar_recv.at[m, w])
             total = s1buf[m, coord(2 * d, True)].astype(F32) + r1buf[m, w, 0].astype(F32)
             aggbuf[m, w] = total.astype(BF16)
             part = half_of(w)
@@ -293,11 +292,12 @@
             total = total + r1buf[m, w, 0, part].astype(F32) + rhalf[m, w].astype(F32)
             aggbuf[m, w, part] = total.astype(BF16)
             a_agg(m, d, w).start()
+    kv[2].start()
     for m in order:
         total = s1buf[m, a1].astype(F32)
-        for stage, kind in ((a_direct, 1), (a_agg, 2)):
-            for d, w in ways:
-                stage(m, d, w).wait_recv()
+        await_bytes(r1buf.at[m, :, pl.ds(1, 2)], ad_recv.at[m])
+        for kind in (1, 2):
+            for w in range(2):
                 total = total + r1buf[m, w, kind].astype(F32)
         s2buf[:, m] = total.astype(BF16)
     def b_start(d):
@@ -305,11 +305,11 @@
         stage_b(d, True).start()
 
     each(b_start)
+    kv[3].start()
     kv[4].start()
     stage_b(0, True).start()
-    stage_b(0, True).wait_recv()
-    each(lambda d: stage_b(d, False).wait_recv())
-    each(lambda d: stage_b(d, True).wait_recv())
+    await_bytes(r2buf.at[pl.ds(1, side - 1)], b_recv)
+    await_bytes(r2sib, c_recv)
     mine = s2buf[a2].astype(F32)
     other = r2sib[0].astype(F32)
     for d in range(1, side):
@@ -325,7 +325,7 @@
             lanes += [use[b * rows:(b + 1) * rows] for b in range(blocks)]
         moment = jnp.concatenate(lanes, axis=1) + (mompad[m] + sibmom[m])
         for r in range(own_rows):
-            newmom_ref[0, m, r:r + 1, :] = jnp.where(
+            mombuf[0, m, r:r + 1, :] = jnp.where(
                 core == 0, moment[r:r + 1], moment[own_rows + r:own_rows + r + 1]
             )
         wide = fast_ref[0, m, pl.ds(base_row, pair * rows), :].astype(F32)
@@ -339,18 +339,30 @@
         fresh = jnp.where(core == 0, fresh[:, :half], fresh[:, half:])
         parts = [fresh[:, b * LANES:(b + 1) * LANES] for b in range(blocks)]
         packed = jnp.concatenate(parts, axis=0) if blocks > 1 else parts[0]
-        rbuf[core, a1, a2, m] = packed.astype(BF16)
+        rbuf[core, a1, PLACE[0], m] = packed.astype(BF16)
 
     def g_first(d):
-        spot = rbuf.at[core, a1, a2]
-        return remote(spot, spot, g1_send.at[d - 1], g1_recv.at[d - 1], along(d, False))
-
-    def g_second(kind, d, w):
-        return second(rbuf, g2_send, g2_recv, kind, d, w)
+        return remote(
+            rbuf.at[core, a1, PLACE[0]], rbuf.at[core, a1, PLACE[side - d]],
+            send_sem.at[2], g1_recv.at[min(min(d, side - d), 3) - 1], along(d, False),
+        )
+
+    def g_step(g, kind, d, w):
+        low, count = ACROSS[g][w] if kind == 3 else GROUPS[g]
+        origin = a1 if kind < 2 else coord(2 * (side - d), True)
+        reach = d if kind in (1, 2) else 2 * d
+        slab = rbuf.at[core, origin, pl.ds(low, count)]
+        spot = (g * 2 + w, 6 + w, 8 + w, 10)[kind]
+        return remote(slab, slab, send_sem.at[1], gr_recv.at[spot], along(reach, True))
+
+    def g_steps(kind):
+        return [
+            (g, kind, d, w) for g in range(3) for d, w in ways if kind < 3 or ACROSS[g][w]
+        ]
 
     def g_sib(n):
         slab = rbuf.at[core, coord(n, True)]
-        return remote(slab, slab, gs_send.at[n], gs_recv.at[n], sibling)
+        return remote(slab, slab, send_sem.at[3], gs_recv, sibling)
 
     def spread(fn):
         for kind in (0, 1):
@@ -374,25 +386,24 @@
         for d, w in ways:
             fn(2, d, w).wait_recv()
             sib((side - 3 * d) % side).start()
-        for d, w in ways:
-            fn(3, d, w).wait_recv()
+        await_bytes(wbuf.at[0, 0], w2_recv.at[6])
         sib(side // 2).start()
 
-    def await_sib(sib):
-        lax.fori_loop(0, side, lambda n, _: (sib(n).wait_recv(), 0)[1], 0)
-
-    each(lambda d: g_first(d).start())
+    newmom_copy = pltpu.make_async_copy(mombuf, newmom_ref, out_sem.at[1])
+    for d in range(1, side):
+        g_first(d).start()
     kv[5].start()
-    each(lambda d: g_first(d).wait_recv())
-    spread(g_second)
-    for copy in kv[6:]:
-        copy.start()
-
-    relay_far(g_second)
-    hand_near(g_second, g_sib)
+    for g, steps in enumerate(GROUP_STEPS):
+        low, count = (0, steps) if g else (1, steps)
+        await_bytes(rbuf.at[core, a1, pl.ds(low, count)], g1_recv.at[g])
+        for kind in (0, 1):
+            for d, w in ways:
+                g_step(g, kind, d, w).start()
+    g_sib(0).start()
+
+    newmom_copy.start()
     loads[3].wait()
-    for copy in kv:
-        copy.wait_recv()
+    await_bytes(ext_k.at[pl.ds(0, tok)], kv_recv.at[0])
     chunk = tok // 4
     span = tok + chunk
     scale = 1.0 / math.sqrt(hd)
@@ -400,7 +411,7 @@
     k_local = lax.broadcasted_iota(jnp.int32, (chunk, span), 1)
     window = (k_local > q_local) & (k_local <= q_local + tok)
 
-    def attend(i, _):
+    def score(i, _):
         part = pl.ds(pl.multiple_of(i * chunk, chunk), chunk)
         reach = pl.ds(pl.multiple_of(i * chunk, chunk), span)
         first_key = jnp.where(seq == 0, tok, 0) - i * chunk
@@ -408,57 +419,102 @@
         scores = jnp.where(window & (k_local >= first_key), scores, NEG_LARGE)
         highest = jnp.max(scores, axis=1, keepdims=True)
         expo = jnp.exp(scores - highest)
-        total = jnp.sum(expo, axis=1, keepdims=True)
-        att[part, :] = nn(expo.astype(BF16), ext_v[reach, :]) / total
+        sums[part, :] = jnp.sum(expo, axis=1, keepdims=True)
+        ebuf[i] = expo.astype(BF16)
         return 0
 
+    lax.fori_loop(0, 4, score, 0)
+
+    def attend(i, _):
+        part = pl.ds(pl.multiple_of(i * chunk, chunk), chunk)
+        reach = pl.ds(pl.multiple_of(i * chunk, chunk), span)
+        att[part, :] = nn(ebuf[i], ext_v[reach, :]) / sums[part, :]
+        return 0
+
+    for g in range(3):
+        for d, w in ways:
+            g_step(g, 0, d, w).wait_recv()
+            if ACROSS[g][w]:
+                g_step(g, 3, d, w).start()
+            g_step(g, 2, d, w).start()
+    for copy in kv[6:]:
+        copy.start()
+    for d, w in ways:
+        g_sib((side - 2 * d) % side).start()
+    for d, w in ways:
+        await_bytes(rbuf.at[0, 0], gr_recv.at[6 + w])
+        g_sib(side - d).start()
+    for d, w in ways:
+        await_bytes(rbuf.at[0, 0], gr_recv.at[8 + w])
+        g_sib((side - 3 * d) % side).start()
+    await_bytes(rbuf.at[0, 0], gr_recv.at[10])
+    g_sib(side // 2).start()
+    await_bytes(wbuf.at[0, 0, pl.ds(0, side - 1)], w1_recv)
+    spread(w_second)
+    await_bytes(ext_v.at[pl.ds(0, tok)], kv_recv.at[1])
     lax.fori_loop(0, 4, attend, 0)
 
-    hand_far(g_second, g_sib)
-    each(lambda d: w_first(d).wait_recv())
-    spread(w_second)
-    await_sib(g_sib)
-
-    def unpack(py, _):
-        for m in range(3):
-            lanes = []
-            for h in range(2):
-                tile = (rbuf[0, py, :, m] if h == 0 else rbuf[1, :, py, m]).astype(F32)
-                lanes += [
-                    tile[:, b * rows:(b + 1) * rows].reshape(side * rows, LANES) for b in range(blocks)
-                ]
-            place = pl.ds(pl.multiple_of(py * side * rows, side * rows), side * rows)
-            renewed[m, place, :] = jnp.concatenate(lanes, axis=1).astype(BF16)
-        return 0
-
-    lax.fori_loop(0, side, unpack, 0)
+    def unpack(h):
+        def body(py, _):
+            for m in range(3):
+                pieces = []
+                for pz in range(side):
+                    line, turn = (py, lax.rem(pz + side - z, side)) if h == 0 else (pz, lax.rem(py + side - y, side))
+                    place = sum(jnp.where(turn == t, p, 0) for t, p in PLACE.items())
+                    tile = rbuf[h, line, place, m].astype(F32)
+                    lanes = [tile[b * rows:(b + 1) * rows] for b in range(blocks)]
+                    pieces.append(jnp.concatenate(lanes, axis=1))
+                part = pl.ds(pl.multiple_of(py * side * rows, side * rows), side * rows)
+                renewed[m, part, h * half:(h + 1) * half] = jnp.concatenate(pieces, axis=0).astype(BF16)
+            return 0
+
+        lax.fori_loop(0, side, body, 0)
+
+    for h in range(2):
+        @pl.when(core == h)
+        def _():
+            unpack(h)
+
+    await_bytes(rbuf.at[0], gs_recv)
+    for h in range(2):
+        @pl.when(core != h)
+        def _():
+            unpack(h)
 
     def to_right(i):
         piece = comb.at[head, pl.ds(pl.multiple_of(i * chunk, chunk), chunk)]
-        return remote(piece, piece, x_send.at[0, i], x_recv.at[0, i], right)
+        return remote(piece, piece, send_sem.at[4], x_recv.at[0, i], right)
 
     def to_left(i):
         piece = comb.at[head, pl.ds(pl.multiple_of(i * chunk, chunk), chunk)]
-        return remote(piece, piece, x_send.at[1, i], x_recv.at[1, i], left)
+        return remote(piece, piece, send_sem.at[4], x_recv.at[1, i], left)
 
     def forward(i, way):
         source = lax.rem(head + (heads - 1 if way == 0 else 1), heads)
         piece = comb.at[source, pl.ds(pl.multiple_of(i * chunk, chunk), chunk)]
-        return remote(piece, piece, f_send.at[i], f_recv.at[i], right if way == 0 else left)
-
-    def produce(n, _):
-        i = 2 * lax.rem(n, 2) + lax.div(n, 2)
+        return remote(piece, piece, send_sem.at[5], f_recv.at[i], right if way == 0 else left)
+
+    def produce(i, first):
         part = pl.ds(pl.multiple_of(i * chunk, chunk), chunk)
         gate = nt(q_ref[part, :], renewed[0])
         up = nt(q_ref[part, :], renewed[1])
         fast_in = (gate * jax.nn.sigmoid(gate) * up).astype(BF16)
         fast_out = nt(fast_in, renewed[2])
         comb[head, part, :] = (att[part, :] + fast_out).astype(BF16)
-        to_right(i).start()
-        to_left(i).start()
+        if first:
+            to_right(i).start()
+        else:
+            to_left(i).start()
+
+    def produce_pair(n, _):
+        produce(n, True)
+        produce(n + 2, False)
         return 0
 
-    lax.fori_loop(0, 4, produce, 0)
+    lax.fori_loop(0, 2, produce_pair, 0)
+    for n in range(2):
+        to_right(n + 2).start()
+        to_left(n).start()
 
     def pass_on(n):
         to_right(n).wait_recv()
@@ -470,7 +526,7 @@
     hand_near(w_second, w_sib)
     pass_on(0)
     hand_far(w_second, w_sib)
-    await_sib(w_sib)
+    await_bytes(wbuf.at[0], ws_recv)
     pass_on(1)
     w_rows = wbuf.shape[3]
 
@@ -482,6 +538,10 @@
         return 0
 
     lax.fori_loop(0, side, natural, 0)
+
+    def out_copy(i):
+        part = pl.ds(pl.multiple_of(i * chunk, chunk), chunk)
+        return pltpu.make_async_copy(outbuf.at[part], out_ref.at[part], out_sem.at[0])
 
     def project(source, i, first=False, last=False):
         part = pl.ds(pl.multiple_of(i * chunk, chunk), chunk)
@@ -490,7 +550,8 @@
         if not first:
             value = acc[part, :] + value
         if last:
-            out_ref[part, :] = value.astype(BF16)
+            outbuf[part, :] = value.astype(BF16)
+            out_copy(i).start()
         else:
             acc[part, :] = value
 
@@ -522,44 +583,21 @@
 
     lax.fori_loop(0, 2, finish, 0)
 
-    for copy in kv + [mom_copy, ex_down()]:
-        copy.wait_send()
-    for m in range(2):
-        for p in range(2):
-            ex_part(m, p, 1).wait_send()
-
-    def drain(d):
-        stage_b(d, False).wait_send()
-        stage_b(d, True).wait_send()
-        g_first(d).wait_send()
-        w_first(d).wait_send()
-
-    each(drain)
-    stage_b(0, True).wait_send()
-    for d, w in ways:
-        for m in range(3):
-            for stage in (a_half, a_relay, a_direct, a_agg):
-                stage(m, d, w).wait_send()
-        for kind in range(4):
-            g_second(kind, d, w).wait_send()
-            w_second(kind, d, w).wait_send()
-
-    def drain_sib(d, _):
-        g_sib(d).wait_send()
-        w_sib(d).wait_send()
-        return 0
-
-    lax.fori_loop(0, side, drain_sib, 0)
-
-    def drain_x(n, _):
-        for i in (n, n + 2):
-            to_right(i).wait_send()
-            to_left(i).wait_send()
-        forward(n, 0).wait_send()
-        forward(n + 2, 1).wait_send()
-        return 0
-
-    lax.fori_loop(0, 2, drain_x, 0)
+    newmom_copy.wait()
+    pltpu.make_async_copy(outbuf, out_ref, out_sem.at[0]).wait()
+    slab = side * tall * LANES
+    size = {
+        0: 3 * (half * hd) + 3 * 7 * slab + side * 3 * tall * LANES + 2 * 3 * rows * hd,
+        1: 2 * tok * hd + 7 * 3 * slab,
+        3: 3 * side * slab + (side - 1) * w_rows * hd + 7 * side * w_rows * hd,
+        4: side * side * w_rows * hd + 2 * tok * hd,
+        5: tok * hd,
+    }
+    for n, count in size.items():
+        part = wnat.at[pl.ds(0, count // hd)]
+        remote(part, part, send_sem.at[n], mom_recv, sibling).wait_send()
+    part = rbuf.at[0, pl.ds(0, 2), pl.ds(0, side - 1)]
+    remote(part, part, send_sem.at[2], mom_recv, sibling).wait_send()
 
 
 def shards(side, queries, keys, values, rates, fast, momentum, out_proj):
@@ -575,7 +613,6 @@
     dma = pltpu.SemaphoreType.DMA
     peers = side - 1
     anywhere = pl.BlockSpec(memory_space=pl.ANY)
-    vmem = pl.BlockSpec(memory_space=pltpu.VMEM)
     return tuple(pl.pallas_call(
         functools.partial(layer_kernel, side, heads, grad_scale),
         out_shape=(
@@ -583,7 +620,7 @@
             pltpu.VMEM(momentum.shape, F32),
         ),
         in_specs=[anywhere] * 7,
-        out_specs=(vmem, vmem),
+        out_specs=(anywhere, anywhere),
         scratch_shapes=[
             pltpu.VMEM((1, tok), F32),
             pltpu.VMEM(momentum.shape, F32),
@@ -611,11 +648,12 @@
             pltpu.VMEM((tok, hd), F32),
             pltpu.VMEM((heads, tok, hd), BF16),
             pltpu.VMEM((tok, hd), F32),
-            dma((7,)), dma((5,)), dma((5,)), dma((2, 4)), dma((2, 4)), dma(()), dma(()),
-            dma((3, 2, 4)), dma((3, 2, 4)), dma((side,)), dma((side,)), dma((side,)), dma((side,)),
-            dma((peers,)), dma((peers,)), dma((4, 2)), dma((4, 2)), dma((side,)), dma((side,)),
-            dma((peers,)), dma((peers,)), dma((4, 2)), dma((4, 2)), dma((side,)), dma((side,)),
-            dma((2, 4)), dma((2, 4)), dma((4,)), dma((4,)),
+            pltpu.VMEM((4, tok // 4, tok + tok // 4), BF16),
+            pltpu.VMEM((tok, 1), F32),
+            pltpu.VMEM((tok, hd), BF16),
+            pltpu.VMEM(momentum.shape, F32),
+            dma((7,)), dma((6,)), dma((3,)), dma((2,)), dma(()), dma((3, 2)), dma((3,)), dma(()), dma(()),
+            dma((3,)), dma((11,)), dma(()), dma(()), dma((7,)), dma(()), dma((2, 4)), dma((4,)), dma((2,)),
         ],
         compiler_params=pltpu.CompilerParams(
             collective_id=0, has_side_effects=True, vmem_limit_bytes=56 * 1024 * 1024,

time: 78.2 us -> 74.6 us (0.954)
  the two profiles are of different devices: /device:TPU:1 before, /device:TPU:64 now
where the time goes in v3:
time: 74.6 us; the launch traced here: 74.4 us
  Pallas kernels  72.4 us (97%)
  local copies, waits for them, and re-layouts  1.4 us (2%)
    pallas_call x1, Pallas kernels, shards(): pl.pallas_call(functools.partial(layer_kernel, side, heads, grad_scale),...  72.4 us

profile of v3, /device:TPU:64, one launch (start us, length us, event | category | flops | bytes accessed | tf_op | source)
XLA Modules:
  0.0 74.4 jit_solution(13081372674129481975)
XLA Ops:
  0.6 72.4 %shard_map.86 = (bf16[512,512]{1,0:T(8,128)(2,1)S(1)}, f32[1,3,4,512]{3,2,1,0:T(4,128)S(1)}) custom-call(bf16[512,512]{1,0:T(8,128)(2,1)} %q_hbm.1, bf16[512,512]{1,0:T(8,128)(2,1)} %k_hbm.1, bf16[512,512]{1,0:T(8,128)(2,1)} %v_hbm.1, f32[1,512]{1,0:T(1,128)} %bitcast.1, bf16[1,3,512,512]{3,2,1,0:T(8,128)(2,1)} %fast_hbm.1, f32[1,3,4,512]{3,2,1,0:T(4,128)} %mom_hbm.1, ...), custom_call_target="tpu_custom_call" | custom-call | tf_op jit(solution)/shard_map/pallas_call | solution.py:616
  73.0 0.8 %copy.11 = bf16[512,512]{1,0:T(8,128)(2,1)} copy(bf16[512,512]{1,0:T(8,128)(2,1)S(1)} %get-tuple-element.2) | data formatting | bytes 1048576
  73.8 0.6 copy.12

commit v4 on v3

--- a/solution.py
+++ b/solution.py
@@ -38,7 +38,7 @@
     q_hbm, k_hbm, v_hbm, rates_hbm, fast_hbm, mom_hbm, proj_hbm,
     out_ref, newmom_ref,
     rates_ref, mom_ref, q_ref, fast_ref, ext_k, ext_v, err_t, grads, gbuf, exbuf, s1buf, r1buf, rhalf, aggbuf, s2buf, r2buf,
-    r2sib, mompad, sibmom, rbuf, renewed, wbuf, wnat, att, comb, acc, ebuf, sums, outbuf, mombuf,
+    r2sib, mompad, sibmom, rbuf, renewed, wbuf, wnat, att, comb, acc, outbuf, mombuf,
     load_sem, send_sem, ex_recv, kv_recv, mom_recv, ar_recv, ad_recv, b_recv, c_recv,
     g1_recv, gr_recv, gs_recv, w1_recv, w2_recv, ws_recv, x_recv, f_recv, out_sem,
 ):
@@ -81,15 +81,16 @@
 
     loads = [
         pltpu.make_async_copy(k_hbm, ext_k.at[pl.ds(tok, tok)], load_sem.at[0]),
-        pltpu.make_async_copy(fast_hbm, fast_ref, load_sem.at[1]),
+        pltpu.make_async_copy(fast_hbm.at[:, pl.ds(0, 2)], fast_ref.at[:, pl.ds(0, 2)], load_sem.at[1]),
         pltpu.make_async_copy(v_hbm, ext_v.at[pl.ds(tok, tok)], load_sem.at[2]),
         pltpu.make_async_copy(q_hbm, q_ref, load_sem.at[3]),
         pltpu.make_async_copy(proj_hbm, wbuf.at[core, a1, a2], load_sem.at[4]),
         pltpu.make_async_copy(mom_hbm, mom_ref, load_sem.at[5]),
         pltpu.make_async_copy(rates_hbm, rates_ref, load_sem.at[6]),
+        pltpu.make_async_copy(fast_hbm.at[:, pl.ds(2, 1)], fast_ref.at[:, pl.ds(2, 1)], load_sem.at[7]),
     ]
-    for load in (loads[0], loads[1], loads[2], loads[6], loads[5], loads[4], loads[3]):
-        load.start()
+    for n in (0, 1, 6, 2, 7, 5, 4, 3):
+        loads[n].start()
 
     def await_bytes(ref, sem):
         remote(ref, ref, send_sem.at[0], sem, sibling).wait_recv()
@@ -107,8 +108,8 @@
     for device in (sibling, right, left, far):
         pl.semaphore_signal(barrier, inc=1, device_id=device, device_id_type=MESH)
 
-    for load in (loads[0], loads[1], loads[2], loads[6]):
-        load.wait()
+    for n in (0, 1, 6, 2, 7):
+        loads[n].wait()
 
     def gradient(i, first):
         part = pl.ds(pl.multiple_of(i * half, half), half)
@@ -211,9 +212,9 @@
     kv = [
         remote(
             ext.at[pl.ds(tok + n * kv_rows, kv_rows)], ext.at[pl.ds(n * kv_rows, kv_rows)],
-            send_sem.at[1], kv_recv.at[i], after,
-        )
-        for i, ext in enumerate((ext_k, ext_v)) for n in range(4)
+            send_sem.at[1], kv_recv.at[i, n], after,
+        )
+        for n in (3, 2, 1, 0) for i, ext in enumerate((ext_k, ext_v))
     ]
     for copy in kv[:2]:
         copy.start()
@@ -264,10 +265,10 @@
             send_sem.at[0], ad_recv.at[m], along(2 * d, True),
         )
 
-    def stage_b(d, swap):
+    def stage_b(m, d, swap):
         send, recv = (send_sem.at[0], c_recv) if swap else (send_sem.at[2], b_recv)
         return remote(
-            s2buf.at[coord(d, False)], (r2sib if swap else r2buf).at[d],
+            s2buf.at[coord(d, False), m], (r2sib if swap else r2buf).at[d, m],
             send, recv, along(d, False, swap),
         )
 
@@ -292,7 +293,6 @@
             total = total + r1buf[m, w, 0, part].astype(F32) + rhalf[m, w].astype(F32)
             aggbuf[m, w, part] = total.astype(BF16)
             a_agg(m, d, w).start()
-    kv[2].start()
     for m in order:
         total = s1buf[m, a1].astype(F32)
         await_bytes(r1buf.at[m, :, pl.ds(1, 2)], ad_recv.at[m])
@@ -300,14 +300,13 @@
             for w in range(2):
                 total = total + r1buf[m, w, kind].astype(F32)
         s2buf[:, m] = total.astype(BF16)
-    def b_start(d):
-        stage_b(d, False).start()
-        stage_b(d, True).start()
-
-    each(b_start)
-    kv[3].start()
-    kv[4].start()
-    stage_b(0, True).start()
+
+        def b_start(d, m=m):
+            stage_b(m, d, False).start()
+            stage_b(m, d, True).start()
+
+        each(b_start)
+        stage_b(m, 0, True).start()
     await_bytes(r2buf.at[pl.ds(1, side - 1)], b_recv)
     await_bytes(r2sib, c_recv)
     mine = s2buf[a2].astype(F32)
@@ -349,8 +348,9 @@
 
     def g_step(g, kind, d, w):
         low, count = ACROSS[g][w] if kind == 3 else GROUPS[g]
-        origin = a1 if kind < 2 else coord(2 * (side - d), True)
-        reach = d if kind in (1, 2) else 2 * d
+        direct = kind == 2 and g == 2
+        origin = a1 if kind < 2 or direct else coord(2 * (side - d), True)
+        reach = 3 * d if direct else d if kind in (1, 2) else 2 * d
         slab = rbuf.at[core, origin, pl.ds(low, count)]
         spot = (g * 2 + w, 6 + w, 8 + w, 10)[kind]
         return remote(slab, slab, send_sem.at[1], gr_recv.at[spot], along(reach, True))
@@ -392,18 +392,16 @@
     newmom_copy = pltpu.make_async_copy(mombuf, newmom_ref, out_sem.at[1])
     for d in range(1, side):
         g_first(d).start()
-    kv[5].start()
     for g, steps in enumerate(GROUP_STEPS):
         low, count = (0, steps) if g else (1, steps)
         await_bytes(rbuf.at[core, a1, pl.ds(low, count)], g1_recv.at[g])
-        for kind in (0, 1):
+        for kind in (0, 2, 1) if g == 2 else (0, 1):
             for d, w in ways:
                 g_step(g, kind, d, w).start()
     g_sib(0).start()
 
     newmom_copy.start()
     loads[3].wait()
-    await_bytes(ext_k.at[pl.ds(0, tok)], kv_recv.at[0])
     chunk = tok // 4
     span = tok + chunk
     scale = 1.0 / math.sqrt(hd)
@@ -411,33 +409,29 @@
     k_local = lax.broadcasted_iota(jnp.int32, (chunk, span), 1)
     window = (k_local > q_local) & (k_local <= q_local + tok)
 
-    def score(i, _):
-        part = pl.ds(pl.multiple_of(i * chunk, chunk), chunk)
-        reach = pl.ds(pl.multiple_of(i * chunk, chunk), span)
-        first_key = jnp.where(seq == 0, tok, 0) - i * chunk
+    def attend(n):
+        for i in range(2):
+            kv[2 * (3 - n) + i].wait_recv()
+        part = pl.ds(n * chunk, chunk)
+        reach = pl.ds(n * chunk, span)
+        first_key = jnp.where(seq == 0, tok, 0) - n * chunk
         scores = nt(q_ref[part, :], ext_k[reach, :]) * scale
         scores = jnp.where(window & (k_local >= first_key), scores, NEG_LARGE)
         highest = jnp.max(scores, axis=1, keepdims=True)
         expo = jnp.exp(scores - highest)
-        sums[part, :] = jnp.sum(expo, axis=1, keepdims=True)
-        ebuf[i] = expo.astype(BF16)
-        return 0
-
-    lax.fori_loop(0, 4, score, 0)
-
-    def attend(i, _):
-        part = pl.ds(pl.multiple_of(i * chunk, chunk), chunk)
-        reach = pl.ds(pl.multiple_of(i * chunk, chunk), span)
-        att[part, :] = nn(ebuf[i], ext_v[reach, :]) / sums[part, :]
-        return 0
+        total = jnp.sum(expo, axis=1, keepdims=True)
+        att[part, :] = nn(expo.astype(BF16), ext_v[reach, :]) / total
+
+    attend(3)
 
     for g in range(3):
         for d, w in ways:
             g_step(g, 0, d, w).wait_recv()
             if ACROSS[g][w]:
                 g_step(g, 3, d, w).start()
-            g_step(g, 2, d, w).start()
-    for copy in kv[6:]:
+            if g < 2:
+                g_step(g, 2, d, w).start()
+    for copy in kv[2:]:
         copy.start()
     for d, w in ways:
         g_sib((side - 2 * d) % side).start()
@@ -449,11 +443,6 @@
         g_sib((side - 3 * d) % side).start()
     await_bytes(rbuf.at[0, 0], gr_recv.at[10])
     g_sib(side // 2).start()
-    await_bytes(wbuf.at[0, 0, pl.ds(0, side - 1)], w1_recv)
-    spread(w_second)
-    await_bytes(ext_v.at[pl.ds(0, tok)], kv_recv.at[1])
-    lax.fori_loop(0, 4, attend, 0)
-
     def unpack(h):
         def body(py, _):
             for m in range(3):
@@ -494,40 +483,57 @@
         piece = comb.at[source, pl.ds(pl.multiple_of(i * chunk, chunk), chunk)]
         return remote(piece, piece, send_sem.at[5], f_recv.at[i], right if way == 0 else left)
 
-    def produce(i, first):
-        part = pl.ds(pl.multiple_of(i * chunk, chunk), chunk)
+    def produce(i):
+        part = pl.ds(i * chunk, chunk)
         gate = nt(q_ref[part, :], renewed[0])
         up = nt(q_ref[part, :], renewed[1])
         fast_in = (gate * jax.nn.sigmoid(gate) * up).astype(BF16)
         fast_out = nt(fast_in, renewed[2])
         comb[head, part, :] = (att[part, :] + fast_out).astype(BF16)
-        if first:
-            to_right(i).start()
+
+    inner = (core == 1) | ((z > 0) & (z < side - 1))
+
+    def start_w(early):
+        @pl.when(inner if early else jnp.logical_not(inner))
+        def _():
+            await_bytes(wbuf.at[0, 0, pl.ds(0, side - 1)], w1_recv)
+            spread(w_second)
+
+    for n in (3, 2, 1, 0):
+        if n < 3:
+            attend(n)
+        produce(n)
+        if n == 3:
+            to_right(3).start()
+            to_left(3).start()
+            start_w(True)
+        elif n == 2:
+            to_left(2).start()
+        elif n == 1:
+            to_right(1).start()
+            to_right(2).start()
+            start_w(False)
         else:
-            to_left(i).start()
-
-    def produce_pair(n, _):
-        produce(n, True)
-        produce(n + 2, False)
-        return 0
-
-    lax.fori_loop(0, 2, produce_pair, 0)
-    for n in range(2):
-        to_right(n + 2).start()
-        to_left(n).start()
+            to_left(0).start()
+            to_left(1).start()
+            to_right(0).start()
 
     def pass_on(n):
-        to_right(n).wait_recv()
-        forward(n, 0).start()
-        to_left(n + 2).wait_recv()
-        forward(n + 2, 1).start()
-
+        if n % 2:
+            to_right(n).wait_recv()
+            forward(n, 0).start()
+        else:
+            to_left(n).wait_recv()
+            forward(n, 1).start()
+
+    pass_on(3)
     relay_far(w_second)
+    pass_on(2)
     hand_near(w_second, w_sib)
+    pass_on(1)
+    hand_far(w_second, w_sib)
     pass_on(0)
-    hand_far(w_second, w_sib)
     await_bytes(wbuf.at[0], ws_recv)
-    pass_on(1)
     w_rows = wbuf.shape[3]
 
     def natural(py, _):
@@ -561,28 +567,13 @@
     from_right = lax.rem(head + 1, heads)
     opposite = lax.rem(head + 2, heads)
 
-    def neighbours(n, _):
-        low = n
-        high = n + 2
-        to_left(low).wait_recv()
-        project(from_left, low)
-        project(from_right, low)
-        to_right(high).wait_recv()
-        project(from_left, high)
-        project(from_right, high)
-        return 0
-
-    lax.fori_loop(0, 2, neighbours, 0)
-
-    def finish(n, _):
-        forward(n, 0).wait_recv()
+    for n in (3, 2, 1, 0):
+        (to_left if n % 2 else to_right)(n).wait_recv()
+        project(from_left, n)
+        project(from_right, n)
+    for n in (3, 2, 1, 0):
+        forward(n, 1 - n % 2).wait_recv()
         project(opposite, n, last=True)
-        forward(n + 2, 1).wait_recv()
-        project(opposite, n + 2, last=True)
-        return 0
-
-    lax.fori_loop(0, 2, finish, 0)
-
     newmom_copy.wait()
     pltpu.make_async_copy(outbuf, out_ref, out_sem.at[0]).wait()
     slab = side * tall * LANES
@@ -648,11 +639,9 @@
             pltpu.VMEM((tok, hd), F32),
             pltpu.VMEM((heads, tok, hd), BF16),
             pltpu.VMEM((tok, hd), F32),
-            pltpu.VMEM((4, tok // 4, tok + tok // 4), BF16),
-            pltpu.VMEM((tok, 1), F32),
             pltpu.VMEM((tok, hd), BF16),
             pltpu.VMEM(momentum.shape, F32),
-            dma((7,)), dma((6,)), dma((3,)), dma((2,)), dma(()), dma((3, 2)), dma((3,)), dma(()), dma(()),
+            dma((8,)), dma((6,)), dma((3,)), dma((2, 4)), dma(()), dma((3, 2)), dma((3,)), dma(()), dma(()),
             dma((3,)), dma((11,)), dma(()), dma(()), dma((7,)), dma(()), dma((2, 4)), dma((4,)), dma((2,)),
         ],
         compiler_params=pltpu.CompilerParams(

time: 74.6 us -> 72.5 us (0.972)
  the two profiles are of different devices: /device:TPU:64 before, /device:TPU:1 now
where the time goes in v4:
time: 72.5 us; the launch traced here: 72.3 us
  Pallas kernels  70.3 us (97%)
  local copies, waits for them, and re-layouts  1.4 us (2%)
    pallas_call x1, Pallas kernels, shards(): pl.pallas_call(functools.partial(layer_kernel, side, heads, grad_scale),...  70.3 us

profile of v4, /device:TPU:1, one launch (start us, length us, event | category | flops | bytes accessed | tf_op | source)
XLA Modules:
  0.0 72.3 jit_solution(3042663450394741084)
XLA Ops:
  0.6 70.3 %shard_map.86 = (bf16[512,512]{1,0:T(8,128)(2,1)S(1)}, f32[1,3,4,512]{3,2,1,0:T(4,128)S(1)}) custom-call(bf16[512,512]{1,0:T(8,128)(2,1)} %q_hbm.1, bf16[512,512]{1,0:T(8,128)(2,1)} %k_hbm.1, bf16[512,512]{1,0:T(8,128)(2,1)} %v_hbm.1, f32[1,512]{1,0:T(1,128)} %bitcast.1, bf16[1,3,512,512]{3,2,1,0:T(8,128)(2,1)} %fast_hbm.1, f32[1,3,4,512]{3,2,1,0:T(4,128)} %mom_hbm.1, ...), custom_call_target="tpu_custom_call" | custom-call | tf_op jit(solution)/shard_map/pallas_call | solution.py:607
  70.9 0.8 %copy.11 = bf16[512,512]{1,0:T(8,128)(2,1)} copy(bf16[512,512]{1,0:T(8,128)(2,1)S(1)} %get-tuple-element.2) | data formatting | bytes 1048576
  71.7 0.6 copy.12

commit v5 on v4

--- a/solution.py
+++ b/solution.py
@@ -229,18 +229,6 @@
     pack_rows(core)
     ex_parts(True)
     pack_down(core)
-    loads[5].wait()
-    row_of = lax.broadcasted_iota(jnp.int32, (rows, hd), 0)
-    for m in range(3):
-        padded = jnp.zeros((rows, hd), F32)
-        for r in range(own_rows):
-            value = MOMENTUM_DECAY * mom_ref[0, m, r:r + 1, :]
-            padded = jnp.where(row_of == r + own_rows * core, jnp.broadcast_to(value, (rows, hd)), padded)
-        mompad[m] = padded
-
-    mom_copy = remote(mompad, sibmom, send_sem.at[0], mom_recv, sibling)
-    mom_copy.start()
-
     def a_relay(m, d, w):
         return remote(
             s1buf.at[m, coord(3 * d, True)], r1buf.at[m, w, 0],
@@ -282,6 +270,18 @@
     for m in order:
         for d, w in ways:
             a_direct(m, d, w).start()
+
+    loads[5].wait()
+    row_of = lax.broadcasted_iota(jnp.int32, (rows, hd), 0)
+    for m in range(3):
+        padded = jnp.zeros((rows, hd), F32)
+        for r in range(own_rows):
+            value = MOMENTUM_DECAY * mom_ref[0, m, r:r + 1, :]
+            padded = jnp.where(row_of == r + own_rows * core, jnp.broadcast_to(value, (rows, hd)), padded)
+        mompad[m] = padded
+
+    mom_copy = remote(mompad, sibmom, send_sem.at[0], mom_recv, sibling)
+    mom_copy.start()
 
     for m in order:
         for d, w in ways:
@@ -443,13 +443,18 @@
         g_sib((side - 3 * d) % side).start()
     await_bytes(rbuf.at[0, 0], gr_recv.at[10])
     g_sib(side // 2).start()
+    def place_of(turn):
+        return sum(jnp.where(turn == t, p, 0) for t, p in PLACE.items())
+
     def unpack(h):
+        fixed = [place_of(lax.rem(pz + side - z, side)) for pz in range(side)] if h == 0 else None
+
         def body(py, _):
+            moving = place_of(lax.rem(py + side - y, side)) if h else None
             for m in range(3):
                 pieces = []
                 for pz in range(side):
-                    line, turn = (py, lax.rem(pz + side - z, side)) if h == 0 else (pz, lax.rem(py + side - y, side))
-                    place = sum(jnp.where(turn == t, p, 0) for t, p in PLACE.items())
+                    line, place = (py, fixed[pz]) if h == 0 else (pz, moving)
                     tile = rbuf[h, line, place, m].astype(F32)
                     lanes = [tile[b * rows:(b + 1) * rows] for b in range(blocks)]
                     pieces.append(jnp.concatenate(lanes, axis=1))

time: 72.5 us -> 72.5 us (level)
  no operation moved by 1% of the time
where the time goes in v5:
time: 72.5 us; the launch traced here: 72.4 us
  Pallas kernels  70.4 us (97%)
  local copies, waits for them, and re-layouts  1.4 us (2%)
    pallas_call x1, Pallas kernels, shards(): pl.pallas_call(functools.partial(layer_kernel, side, heads, grad_scale),...  70.4 us

profile of v5, /device:TPU:1, one launch (start us, length us, event | category | flops | bytes accessed | tf_op | source)
XLA Modules:
  0.0 72.4 jit_solution(12763979549859605580)
XLA Ops:
  0.6 70.4 %shard_map.86 = (bf16[512,512]{1,0:T(8,128)(2,1)S(1)}, f32[1,3,4,512]{3,2,1,0:T(4,128)S(1)}) custom-call(bf16[512,512]{1,0:T(8,128)(2,1)} %q_hbm.1, bf16[512,512]{1,0:T(8,128)(2,1)} %k_hbm.1, bf16[512,512]{1,0:T(8,128)(2,1)} %v_hbm.1, f32[1,512]{1,0:T(1,128)} %bitcast.1, bf16[1,3,512,512]{3,2,1,0:T(8,128)(2,1)} %fast_hbm.1, f32[1,3,4,512]{3,2,1,0:T(4,128)} %mom_hbm.1, ...), custom_call_target="tpu_custom_call" | custom-call | tf_op jit(solution)/shard_map/pallas_call | solution.py:612
  71.0 0.8 %copy.11 = bf16[512,512]{1,0:T(8,128)(2,1)} copy(bf16[512,512]{1,0:T(8,128)(2,1)S(1)} %get-tuple-element.2) | data formatting | bytes 1048576
  71.8 0.6 copy.12
